TPU v7x, 256 devices: a whole 4x4x8 slice. The times are simulated.
256 devices in a mesh: dp: 2 (over y_lo), view: 16 (over x, y_hi, core), head: 8 (over z).
Axes of the slice: x: 4, y: 4 (y_hi: 2, y_lo: 2; y = y_hi * 2 + y_lo), z: 8, core: 2. Of those that a mesh axis runs over, the one named last changes fastest.
Arguments:
- normed: bfloat16 [2, 16, 256, 3072], P('dp', 'view'), may hold values from -6 to 6
- queries: bfloat16 [2, 16, 256, 3072], P('dp', 'view', None, 'head'), may hold values from -180 to 180
- saved_keys: bfloat16 [2, 16, 256, 3072], P('dp', 'view', None, 'head'), may hold values from -4.5 to 4.5
- saved_values: bfloat16 [2, 16, 256, 3072], P('dp', 'view', None, 'head'), may hold values from -6 to 6
- output_grad: bfloat16 [2, 16, 256, 3072], P('dp', 'view', None, 'head'), may hold values from -200 to 200
- view_links: int32 [16, 2], P('view'), may hold values from -1 to 15, as said below
- query_weight: bfloat16 [3072, 3072], P(('dp', 'view'), 'head'), may hold values from -0.109375 to 0.109375
- key_weight: bfloat16 [3072, 3072], P(('dp', 'view'), 'head'), may hold values from -0.109375 to 0.109375
- value_weight: bfloat16 [3072, 3072], P(('dp', 'view'), 'head'), may hold values from -0.109375 to 0.109375
Outputs:
- input_grad: bfloat16 [2, 16, 256, 3072], P('dp', 'view', None, 'head')
- grad_query: float32 [3072, 3072], P(('dp', 'view'), 'head')
- grad_key: float32 [3072, 3072], P(('dp', 'view'), 'head')
- grad_value: float32 [3072, 3072], P(('dp', 'view'), 'head')
Inputs may be any that keep to these rules, and one draw needn't show every extreme that they name: `view_links`: row v holds (v - 1) mod 16 or -1 and then (v + 1) mod 16 or -1; -1 marks a link that view v does not attend.
All inputs are finite; a program needn't handle non-finite values.
Results may differ from a plain program's by a relative error of at most 0.0057.
Values may be sent and summed in bfloat16 or wider, within the bound.
A program may use at most 128 MiB of HBM per device.

v0:
```python
import jax
import jax.numpy as jnp
from jax import lax
from jax.sharding import PartitionSpec as P

HD = 128


def shifted(value, axis, steps):
    count = lax.axis_size(axis)
    pairs = [(source, (source + steps) % count) for source in range(count)]
    return lax.ppermute(value, axis, pairs)


def attend(query_rows, grad_rows, blocks, usable, scaling):
    batch_size, length, col_count = query_rows.shape
    heads_here = col_count // HD
    key_heads = blocks[..., :col_count].reshape(batch_size, 3 * length, heads_here, HD)
    value_heads = blocks[..., col_count:].reshape(batch_size, 3 * length, heads_here, HD)
    query_heads = query_rows.reshape(batch_size, length, heads_here, HD)
    grad_heads = grad_rows.reshape(batch_size, length, heads_here, HD)
    scores = (
        jnp.einsum("bshd,bthd->bhst", query_heads, key_heads, preferred_element_type=jnp.float32)
        * scaling
    )
    scores = jnp.where(usable, scores, -1e30)
    largest = jnp.max(scores, axis=-1, keepdims=True)
    powers = jnp.exp(scores - largest)
    attn_probs = powers / jnp.sum(powers, axis=-1, keepdims=True)
    probs_half = attn_probs.astype(jnp.bfloat16)
    prob_grad = jnp.einsum(
        "bshd,bthd->bhst", grad_heads, value_heads, preferred_element_type=jnp.float32
    )
    row_delta = jnp.sum(attn_probs * prob_grad, axis=-1, keepdims=True)
    score_grad = (scaling * attn_probs * (prob_grad - row_delta)).astype(jnp.bfloat16)
    query_grad = jnp.einsum(
        "bhst,bthd->bshd", score_grad, key_heads, preferred_element_type=jnp.float32
    )
    key_grad = jnp.einsum(
        "bhst,bshd->bthd", score_grad, query_heads, preferred_element_type=jnp.float32
    )
    value_grad = jnp.einsum(
        "bhst,bshd->bthd", probs_half, grad_heads, preferred_element_type=jnp.float32
    )
    query_grad = query_grad.reshape(batch_size, length, col_count)
    key_grad = key_grad.reshape(batch_size, 3, length, col_count)
    value_grad = value_grad.reshape(batch_size, 3, length, col_count)
    return (query_grad, jnp.concatenate([key_grad, value_grad], axis=-1))


def body(
    normed,
    queries,
    saved_keys,
    saved_values,
    output_grad,
    view_links,
    query_weight,
    key_weight,
    value_weight,
):
    scaling = HD ** (-0.5)
    batch_size, view_count, length, col_count = queries.shape
    model_width = normed.shape[-1]
    pairs = jnp.concatenate([saved_keys, saved_values], axis=-1)
    from_lower = shifted(pairs, "view", 1)
    from_upper = shifted(pairs, "view", -1)
    extended = jnp.concatenate([from_lower, pairs, from_upper], axis=1)
    block_index = jnp.arange(3 * length) // length
    pair_grads = jnp.zeros(extended.shape, jnp.float32)
    link_flags = view_links[0] >= 0
    usable = jnp.where(
        block_index == 0, link_flags[0], jnp.where(block_index == 2, link_flags[1], True)
    )
    query_grad, block_grad = attend(queries[:, 0], output_grad[:, 0], extended, usable, scaling)
    query_grads = [query_grad]
    pair_grads = pair_grads.at[:, 0:3].add(block_grad)
    row_count = batch_size * view_count * length
    query_half = jnp.stack(query_grads, axis=1).astype(jnp.bfloat16).reshape(row_count, col_count)
    flat_input = normed.reshape(row_count, model_width)
    mean_scale = 1.0 / (lax.axis_size("dp") * batch_size * lax.axis_size("view") * view_count)

    def weight_term(grads_half):
        product = lax.dot_general(
            flat_input, grads_half, (((0,), (0,)), ((), ())), preferred_element_type=jnp.float32
        )
        return product * mean_scale

    grad_query = lax.psum_scatter(
        weight_term(query_half), ("dp", "view"), scatter_dimension=0, tiled=True
    )
    from_lower_grads = shifted(pair_grads[:, -1:], "view", 1)
    from_upper_grads = shifted(pair_grads[:, :1], "view", -1)
    own_grads = pair_grads[:, 1 : view_count + 1]
    own_grads = own_grads.at[:, :1].add(from_lower_grads)
    own_grads = own_grads.at[:, -1:].add(from_upper_grads)
    key_half = own_grads[..., :col_count].astype(jnp.bfloat16).reshape(row_count, col_count)
    value_half = own_grads[..., col_count:].astype(jnp.bfloat16).reshape(row_count, col_count)
    all_grads = jnp.concatenate([query_half, key_half, value_half], axis=-1)
    grads_three = all_grads.reshape(row_count, 3, col_count)
    stacked = jnp.stack([query_weight, key_weight, value_weight])
    partial_input = jnp.einsum(
        "ric,ipc->rp",
        grads_three,
        lax.all_gather(stacked, ("dp", "view"), axis=1, tiled=True),
        preferred_element_type=jnp.float32,
    )
    summed_input = lax.psum_scatter(partial_input, "head", scatter_dimension=1, tiled=True)
    input_grad = summed_input.astype(jnp.bfloat16).reshape(
        batch_size, view_count, length, model_width // lax.axis_size("head")
    )
    grad_key = lax.psum_scatter(
        weight_term(key_half), ("dp", "view"), scatter_dimension=0, tiled=True
    )
    grad_value = lax.psum_scatter(
        weight_term(value_half), ("dp", "view"), scatter_dimension=0, tiled=True
    )
    return (input_grad, grad_query, grad_key, grad_value)


def solution(mesh):
    placed = (
        P("dp", "view", None, None),
        P("dp", "view", None, "head"),
        P("dp", "view", None, "head"),
        P("dp", "view", None, "head"),
        P("dp", "view", None, "head"),
        P("view", None),
        P(("dp", "view"), "head"),
        P(("dp", "view"), "head"),
        P(("dp", "view"), "head"),
    )
    return jax.shard_map(
        body,
        mesh=mesh,
        in_specs=placed,
        out_specs=(
            P("dp", "view", None, "head"),
            P(("dp", "view"), "head"),
            P(("dp", "view"), "head"),
            P(("dp", "view"), "head"),
        ),
        check_vma=False,
    )
```

profile of v0, /device:TPU:1, one launch (start us, length us, event | category | flops | bytes accessed | tf_op | source)
XLA Modules:
  0.0 592.1 jit_solution(8500871352895043883)
XLA Ops:
  7.2 1.8 pad_maximum_fusion.1
  11.0 4.4 collective-permute-start
  16.4 1.7 copy.42
  19.4 1.3 fusion.34
  20.7 3.6 collective-permute-done
  24.3 4.0 collective-permute-done.1
  30.2 2.0 reshape.231
  32.2 2.4 fusion.43
  34.7 2.4 fusion.1
  38.0 2.0 copy.48
  39.9 2.9 reshape.233
  42.8 2.2 convolution_bitcast_fusion.1
  45.0 2.1 copy.50
  47.1 3.0 reshape.234
  50.0 1.5 constant_dynamic-update-slice_fusion.3
  51.8 1.4 fusion.40
  54.2 28.7 %collective-permute-done.2 = f32[1,1,256,768]{3,2,1,0:T(8,128)} collective-permute-done((f32[1,1,256,768]{3,2,1,0:T(8,128)}, f32[1,1,256,768]{3,2,1,0:T(8,128)}, u32[]{:S(2)}, u32[]{:S(2)}) %collective-permute-start.2) | collective-permute-done | bytes 786464 | tf_op jit(solution)/shard_map/ppermute | solution.py:12
  82.9 2.2 collective-permute-done.3
  85.1 1.7 fusion.16
  86.9 9.7 %all-gather.2.cloned.1.call-done = bf16[3,3072,384]{2,1,0:T(8,128)(2,1)} async-done(((bf16[3,96,384]{2,1,0:T(8,128)(2,1)}), bf16[3,3072,384]{2,1,0:T(8,128)(2,1)}) %all-gather.2.cloned.1.call-update) | async-done | bytes 7077904 | tf_op jit(solution)/shard_map/all_gather | solution.py:105
  96.6 6.9 %convolution_bitcast_fusion = f32[256,3072]{1,0:T(8,128)} fusion(bf16[3,3072,384]{2,1,0:T(8,128)(2,1)} %all-gather.2.cloned.1.call-done, bf16[256,1,384]{2,0,1:T(8,128)(2,1)S(1)} %get-tuple-element.81, bf16[256,1,384]{2,0,1:T(8,128)(2,1)S(1)} %get-tuple-element.80, bf16[256,1,384]{2,0,1:T(8,128)(2,1)S(1)} %copy.51), kind=kOutput, calls=%fused_computation.4 | convolution fusion | flops 1812529152 | bytes 10813440 | tf_op jit(solution)/shard_map/ric,ipc->rp/dot_general | solution.py:102
  103.6 3.0 multiply_bitcast_fusion.2
  106.5 6.1 %copy.60 = f32[3072,384]{1,0:T(8,128)} copy(f32[3072,384]{0,1:T(8,128)} %multiply_bitcast_fusion.2) | data formatting | bytes 9437184
  112.7 3.0 multiply_bitcast_fusion.1
  115.7 6.1 %copy.62 = f32[3072,384]{1,0:T(8,128)} copy(f32[3072,384]{0,1:T(8,128)} %multiply_bitcast_fusion.1) | data formatting | bytes 9437184
  121.9 2.9 multiply_bitcast_fusion
  124.9 6.1 %copy.64 = f32[3072,384]{1,0:T(8,128)} copy(f32[3072,384]{0,1:T(8,128)} %multiply_bitcast_fusion) | data formatting | bytes 9437184
  131.0 15.9 %reduce-scatter.11.cloned.1.call-done = f32[256,384]{1,0:T(8,128)} async-done(((f32[256,3072]{1,0:T(8,128)}), f32[256,384]{1,0:T(8,128)}) %reduce-scatter.11.cloned.1.call-update) | async-done | bytes 393232 | tf_op jit(solution)/shard_map/reduce_scatter | solution.py:108
  146.9 1.7 convert_bitcast_fusion
  148.6 145.6 %reduce-scatter.13.cloned.1.call-done = f32[96,384]{1,0:T(8,128)} async-done(((f32[3072,384]{1,0:T(8,128)}), f32[96,384]{1,0:T(8,128)}) %reduce-scatter.13.cloned.1.call-update) | async-done | bytes 147472
  294.2 145.4 %reduce-scatter.15.cloned.1.call-done = f32[96,384]{1,0:T(8,128)} async-done(((f32[3072,384]{1,0:T(8,128)}), f32[96,384]{1,0:T(8,128)}) %reduce-scatter.15.cloned.1.call-update) | async-done | bytes 147472
  439.7 145.9 %reduce-scatter.17.cloned.1.call-done = f32[96,384]{1,0:T(8,128)} async-done(((f32[3072,384]{1,0:T(8,128)}), f32[96,384]{1,0:T(8,128)}) %reduce-scatter.17.cloned.1.call-update) | async-done | bytes 147472
  (40 shorter events, 8.6 us)
Async XLA Ops:
  7.2 96.4 %copy-start = (bf16[1,1,256,3072]{3,2,1,0:T(8,128)(2,1)S(1)}, bf16[1,1,256,3072]{3,2,1,0:T(8,128)(2,1)}, u32[]{:S(2)}) copy-start(bf16[1,1,256,3072]{3,2,1,0:T(8,128)(2,1)} %param.21) | copy-start | bytes 4718596
  7.2 89.4 %all-gather.2.cloned.1.call-start = ((), (), s32[]{:S(2)}) async-start(), calls=%async_computation.4 | async-start | bytes 7299072 | tf_op jit(solution)/shard_map/all_gather | solution.py:105
  9.0 137.9 %reduce-scatter.11.cloned.1.call-start = ((), (), s32[]{:S(2)}) async-start(), calls=%async_computation.5 | async-start | bytes 3538944 | tf_op jit(solution)/shard_map/reduce_scatter | solution.py:108
  11.0 13.3 %collective-permute-start = (bf16[1,1,256,768]{3,2,1,0:T(8,128)(2,1)S(1)}, bf16[1,1,256,768]{3,2,1,0:T(8,128)(2,1)S(1)}, u32[]{:S(2)}, u32[]{:S(2)}) collective-permute-start(bf16[1,1,256,768]{3,2,1,0:T(8,128)(2,1)S(1)} %constant_dynamic-update-slice_fusion), channel_id=1, source_target_pairs={{0,8},{8,16},{16,24},{24,32},{32,40},{40,48},{48,56},{56,64},{64,7... | collective-permute-start | bytes 1179656 | tf_op jit(solution)/shard_map/ppermute | solution.py:12
  15.4 12.9 %collective-permute-start.1 = (bf16[1,1,256,768]{3,2,1,0:T(8,128)(2,1)S(1)}, bf16[1,1,256,768]{3,2,1,0:T(8,128)(2,1)S(1)}, u32[]{:S(2)}, u32[]{:S(2)}) collective-permute-start(bf16[1,1,256,768]{3,2,1,0:T(8,128)(2,1)S(1)} %constant_dynamic-update-slice_fusion), channel_id=1, source_target_pairs={{0,120},{8,0},{16,8},{24,16},{32,24},{40,32},{48,40},{56,48},{64,5... | collective-permute-start | bytes 1179656 | tf_op jit(solution)/shard_map/ppermute | solution.py:12
  32.2 2.5 copy-start.4
  34.7 2.4 copy-start.3
  38.0 4.9 copy-start.5
  50.0 1.6 copy-start.2
  51.7 2.2 copy-start.1
  53.1 29.7 %collective-permute-start.2 = (f32[1,1,256,768]{3,2,1,0:T(8,128)}, f32[1,1,256,768]{3,2,1,0:T(8,128)}, u32[]{:S(2)}, u32[]{:S(2)}) collective-permute-start(f32[1,1,256,768]{3,2,1,0:T(8,128)} %get-tuple-element.76), channel_id=1, source_target_pairs={{0,8},{8,16},{16,24},{24,32},{32,40},{40,48},{48,56},{56,64},{64,7... | collective-permute-start | bytes 2359304 | tf_op jit(solution)/shard_map/ppermute | solution.py:12
  53.2 31.8 %collective-permute-start.3 = (f32[1,1,256,768]{3,2,1,0:T(8,128)}, f32[1,1,256,768]{3,2,1,0:T(8,128)}, u32[]{:S(2)}, u32[]{:S(2)}) collective-permute-start(f32[1,1,256,768]{3,2,1,0:T(8,128)} %get-tuple-element.77), channel_id=1, source_target_pairs={{0,120},{8,0},{16,8},{24,16},{32,24},{40,32},{48,40},{56,48},{64,5... | collective-permute-start | bytes 2359304 | tf_op jit(solution)/shard_map/ppermute | solution.py:12
  103.5 190.7 %reduce-scatter.13.cloned.1.call-start = ((), (), s32[]{:S(2)}) async-start(), calls=%async_computation.6 | async-start | bytes 4866048
  112.6 327.0 %reduce-scatter.15.cloned.1.call-start = ((), (), s32[]{:S(2)}) async-start(), calls=%async_computation.7 | async-start | bytes 4866048
  121.9 463.6 %reduce-scatter.17.cloned.1.call-start = ((), (), s32[]{:S(2)}) async-start(), calls=%async_computation.8 | async-start | bytes 4866048
Sparse Core Ops, SparseCore 0:
  9.8 86.7 all-gather.1
  103.6 43.2 reduce-scatter.10
  150.0 144.1 reduce-scatter.12
  297.2 142.4 reduce-scatter.14
  442.6 142.8 reduce-scatter.16
where the time goes:
time: 596 us; the launch traced here: 592 us
  waiting for transfers between devices  501 us (84%)
  local copies, waits for them, and re-layouts  40.5 us (7%)
  matrix products  23.6 us (4%)
  between operations  13.9 us (2%)
  other arithmetic  7.72 us (1%)
    unnamed x8, waiting for transfers between devices  437 us
    ppermute x4, waiting for transfers between devices, shifted(): return lax.ppermute(value, axis, pairs)  38.5 us
    unnamed x19, local copies, waits for them, and re-layouts  23.7 us
    reduce_scatter x1, waiting for transfers between devices, body(): lax.psum_scatter(partial_input, 'head', scatter_dimension=1, tiled=True)  15.9 us
  transfers between devices with their start and end apart: 9, of which 9 were waited for; matrix products, arithmetic and copies ran while one was open for 11% of the time, Pallas kernels for 0%

commit v1 on v0

v1 whole, which is shorter than its diff:
```python
import functools

import jax
import jax.numpy as jnp
from jax import lax
from jax.experimental import pallas as pl
from jax.experimental.pallas import tpu as pltpu
from jax.sharding import PartitionSpec as P

HD = 128
MESH = pl.DeviceIdType.MESH
F32 = jnp.float32
BF16 = jnp.bfloat16
NT = (((1,), (1,)), ((), ()))
NN = (((1,), (0,)), ((), ()))
TN = (((0,), (0,)), ((), ()))


def dot(a, b, dims):
    return lax.dot_general(a, b, dims, preferred_element_type=F32)


def kernel(
    links, normed, q_ref, k_ref, v_ref, g_ref, wq, wk, wv,
    dx_out, dq_out, dk_out, dv_out,
    kv, wg, nt, ntp, hown, hpar, own, gs, gr, part, ra1, rra, rb, rb1, rrb, zb, zr,
    ssem, rsem, lsem,
):
    length, cols = q_ref.shape
    heads = cols // HD
    rows = wq.shape[0]
    half = rows // 2
    scaling = HD ** (-0.5)
    dp, vw, z = lax.axis_index("dp"), lax.axis_index("view"), lax.axis_index("head")
    nview, nz = 16, 8
    x = lax.div(vw, 4)
    yh = lax.rem(lax.div(vw, 2), 2)
    c = lax.rem(vw, 2)
    y = yh * 2 + dp

    def at(xx, yy, cc, zz):
        return (lax.rem(yy, 2), xx * 4 + lax.div(yy, 2) * 2 + cc, zz)

    def m(value, n):
        return lax.rem(value + n, n)

    x_up, x_dn, x_far = m(x + 1, 4), m(x - 1, 4), m(x + 2, 4)
    y_up, y_dn = m(y + 1, 4), m(y - 1, 4)
    to_x = {1: at(x_up, y, c, z), -1: at(x_dn, y, c, z)}
    to_y = {1: at(x, y_up, c, z), -1: at(x, y_dn, c, z)}
    to_z = {1: (dp, vw, m(z + 1, nz)), -1: (dp, vw, m(z - 1, nz))}
    to_view = {1: (dp, m(vw + 1, nview), z), -1: (dp, m(vw - 1, nview), z)}
    partner = at(x, y, 1 - c, z)

    started = []

    def send(src, dst, device):
        slot = len(started)
        copy = pltpu.make_async_remote_copy(
            src_ref=src, dst_ref=dst, send_sem=ssem.at[slot], recv_sem=rsem.at[slot],
            device_id=device, device_id_type=MESH,
        )
        copy.start()
        started.append(copy)
        return copy

    barrier = pltpu.get_barrier_semaphore()
    for peers in (to_view, to_x, to_y, to_z):
        for step in (1, -1):
            pl.semaphore_signal(barrier, inc=1, device_id=peers[step], device_id_type=MESH)
    yl = dp
    locals_ = []
    for i, w in enumerate((wq, wk, wv)):
        copy = pltpu.make_async_copy(
            w, wg.at[x, yl, yh, c, :, pl.ds(i * cols, cols)], lsem.at[i]
        )
        copy.start()
        locals_.append(copy)
    pl.semaphore_wait(barrier, 8)

    halo = []
    for h in range(heads):
        hs = pl.ds(h * HD, HD)
        copies = []
        for slot, step in ((0, 1), (1, -1)):
            copies.append(send(k_ref.at[:, hs], kv.at[slot, 0, h], to_view[step]))
            copies.append(send(v_ref.at[:, hs], kv.at[slot, 1, h], to_view[step]))
        halo.append(copies)
    for copy in locals_:
        copy.wait()
    mine = wg.at[x, yl, yh, c]
    w_y1 = [send(mine, mine, to_y[s]) for s in (1, -1)]

    def transpose_chunk(i, _):
        chunk = normed[:, pl.ds(pl.multiple_of(i * 4 * rows, 128), 4 * rows)]
        turned = chunk.T.reshape(2, 2, rows, length)
        nt[lax.rem(i, 4), lax.div(i, 4)] = turned
        return 0

    lax.fori_loop(0, 8, transpose_chunk, 0)

    for copy in w_y1:
        copy.wait_recv()
    lo, hi = pl.ds(0, half), pl.ds(half, half)

    def block_y(yy):
        return lax.rem(yy, 2), lax.div(yy, 2)

    a0, a1 = block_y(y_dn)
    b0, b1 = block_y(y_up)
    from_dn = wg.at[x, a0, a1, c, lo]
    from_up = wg.at[x, b0, b1, c, hi]
    w_y2 = [send(from_dn, from_dn, to_y[1]), send(from_up, from_up, to_y[-1])]
    turned_copy = send(nt.at[:, :, :, 1 - c], ntp, partner)

    pen = [
        jnp.where(links[0, 0] >= 0, 0.0, -1e30).astype(F32),
        None,
        jnp.where(links[0, 1] >= 0, 0.0, -1e30).astype(F32),
    ]
    grad_halo = []
    w_x1, w_x2, w_par = [], [], []

    def attention(h):
        hs = slice(h * HD, (h + 1) * HD)
        for copy in halo[h]:
            copy.wait_recv()
        qh, gh = q_ref[:, hs], g_ref[:, hs]
        ks = [kv[0, 0, h], k_ref[:, hs], kv[1, 0, h]]
        vs = [kv[0, 1, h], v_ref[:, hs], kv[1, 1, h]]
        scores = []
        for j in range(3):
            s = dot(qh, ks[j], NT) * scaling
            scores.append(s if pen[j] is None else s + pen[j])
        top = jnp.maximum(jnp.maximum(scores[0], scores[1]), scores[2])
        top = jnp.max(top, axis=-1, keepdims=True)
        powers = [jnp.exp(s - top) for s in scores]
        total = jnp.sum(powers[0] + powers[1] + powers[2], axis=-1, keepdims=True)
        inv = 1.0 / total
        probs = [e * inv for e in powers]
        pgrads = [dot(gh, vj, NT) for vj in vs]
        delta = probs[0] * pgrads[0] + probs[1] * pgrads[1] + probs[2] * pgrads[2]
        delta = jnp.sum(delta, axis=-1, keepdims=True)
        sg = [(scaling * p * (d - delta)).astype(BF16) for p, d in zip(probs, pgrads)]
        query = dot(sg[0], ks[0], NN) + dot(sg[1], ks[1], NN) + dot(sg[2], ks[2], NN)
        hown[:, hs] = query.astype(BF16)
        for j, slot in ((0, 0), (2, 1)):
            gs[slot, h, 0] = dot(sg[j], qh, TN).astype(BF16)
            gs[slot, h, 1] = dot(probs[j].astype(BF16), gh, TN).astype(BF16)
        own[h, 0] = dot(sg[1], qh, TN)
        own[h, 1] = dot(probs[1].astype(BF16), gh, TN)
        grad_halo.append(
            [
                send(gs.at[0, h], gr.at[0, h], to_view[-1]),
                send(gs.at[1, h], gr.at[1, h], to_view[1]),
            ]
        )

    attention(0)
    for copy in w_y2:
        copy.wait_recv()
    column = wg.at[x, :, :, c]
    w_x1 = [send(column, column, to_x[s]) for s in (1, -1)]
    w_par.append(send(column, column, partner))
    for h in range(1, heads):
        attention(h)
        if h == 1:
            for copy in w_x1:
                copy.wait_recv()
            up, dn = wg.at[x_dn, 0, :, c], wg.at[x_up, 1, :, c]
            w_x2 = [send(up, up, to_x[1]), send(dn, dn, to_x[-1])]
            for xx in (x_dn, x_up):
                column = wg.at[xx, :, :, c]
                w_par.append(send(column, column, partner))
    hq = hown.at[:, pl.ds(0, cols)]
    q_copy = send(hq, hpar.at[:, pl.ds(0, cols)], partner)
    for copy in w_x2:
        copy.wait_recv()
    column = wg.at[x_far, :, :, c]
    w_par.append(send(column, column, partner))

    def weight_part(ci, x_first):
        cs = slice(ci * cols, (ci + 1) * cols)

        def step(xx, _):
            for ll in range(2):
                a = jnp.concatenate([nt[xx, ll, 0, c], nt[xx, ll, 1, c]], axis=0)
                b = ntp[xx, ll].reshape(2 * rows, length)
                acc = dot(a, hown[:, cs], NN) + dot(b, hpar[:, cs], NN)
                acc = acc.astype(BF16)
                for hh in range(2):
                    yy = hh * 2 + ll
                    block = acc[hh * rows : (hh + 1) * rows]
                    if x_first:
                        part[ci, xx, yy] = block
                    else:
                        part[ci, yy, xx] = block
            return 0

        lax.fori_loop(0, 4, step, 0)

    class Scatter:
        def __init__(self, ci, pa, to_a, pb, to_b):
            self.ci, self.pa, self.to_a, self.pb, self.to_b = ci, pa, to_a, pb, to_b
            self.aup, self.adn, self.afar = m(pa + 1, 4), m(pa - 1, 4), m(pa + 2, 4)
            self.bup, self.bdn, self.bfar = m(pb + 1, 4), m(pb - 1, 4), m(pb + 2, 4)

        def first(self):
            ci = self.ci
            low, high = pl.ds(0, 2), pl.ds(2, 2)
            self.f1 = [
                send(part.at[ci, self.afar, low], ra1.at[ci, 0], self.to_a[1]),
                send(part.at[ci, self.afar, high], ra1.at[ci, 1], self.to_a[-1]),
            ]
            self.f2 = [
                send(part.at[ci, self.aup, high], rra.at[ci, 0, high], self.to_a[1]),
                send(part.at[ci, self.adn, low], rra.at[ci, 1, low], self.to_a[-1]),
            ]

        def second(self):
            ci = self.ci
            low, high = pl.ds(0, 2), pl.ds(2, 2)
            for i, (block, piece, device) in enumerate(
                ((self.aup, low, self.to_a[1]), (self.adn, high, self.to_a[-1]))
            ):
                self.f1[i].wait_recv()
                old = part[ci, block, piece].astype(F32)
                part[ci, block, piece] = (old + ra1[ci, i].astype(F32)).astype(BF16)
                self.f2.append(send(part.at[ci, block, piece], rra.at[ci, i, piece], device))

        def third(self):
            ci = self.ci
            for copy in self.f2:
                copy.wait_recv()
            for j in range(4):
                value = part[ci, self.pa, j].astype(F32) + rra[ci, 0, j].astype(F32)
                rb[ci, j] = (value + rra[ci, 1, j].astype(F32)).astype(BF16)
            self.g1 = [
                send(rb.at[ci, self.bfar, lo], rb1.at[ci, 0], self.to_b[1]),
                send(rb.at[ci, self.bfar, hi], rb1.at[ci, 1], self.to_b[-1]),
            ]
            self.g2 = [
                send(rb.at[ci, self.bup, hi], rrb.at[ci, 0, hi], self.to_b[1]),
                send(rb.at[ci, self.bdn, lo], rrb.at[ci, 1, lo], self.to_b[-1]),
            ]

        def fourth(self):
            ci = self.ci
            for i, (block, piece, device) in enumerate(
                ((self.bup, lo, self.to_b[1]), (self.bdn, hi, self.to_b[-1]))
            ):
                self.g1[i].wait_recv()
                old = rb[ci, block, piece].astype(F32)
                rb[ci, block, piece] = (old + rb1[ci, i].astype(F32)).astype(BF16)
                self.g2.append(send(rb.at[ci, block, piece], rrb.at[ci, i, piece], device))

        def finish(self, out):
            ci = self.ci
            for copy in self.g2:
                copy.wait_recv()
            value = rb[ci, self.pb].astype(F32) + rrb[ci, 0].astype(F32)
            out[...] = (value + rrb[ci, 1].astype(F32)) * (1.0 / 32.0)

    rs_q = Scatter(0, x, to_x, y, to_y)
    rs_k = Scatter(1, x, to_x, y, to_y)
    rs_v = Scatter(2, y, to_y, x, to_x)

    turned_copy.wait_recv()
    q_copy.wait_recv()
    weight_part(0, True)
    rs_q.first()

    for h in range(heads):
        for copy in grad_halo[h]:
            copy.wait_recv()
        for i in range(2):
            value = own[h, i] + gr[0, h, i].astype(F32) + gr[1, h, i].astype(F32)
            start = (1 + i) * cols + h * HD
            hown[:, start : start + HD] = value.astype(BF16)
    hkv = pl.ds(cols, 2 * cols)
    kv_copy = send(hown.at[:, hkv], hpar.at[:, hkv], partner)
    rs_q.second()
    for copy in w_par:
        copy.wait_recv()

    def input_block(j):
        w = wg[lax.rem(j, 4), lax.div(j, 4)].reshape(4 * rows, 3 * cols)
        return dot(hown[...], w, NT)

    top_half, low_half = pl.ds(0, length // 2), pl.ds(length // 2, length // 2)
    far = m(z + 4, nz)
    zb[far] = input_block(far).astype(BF16)
    zs = [[
        send(zb.at[far, top_half], zr.at[0, 0, top_half], to_z[1]),
        send(zb.at[far, low_half], zr.at[1, 0, low_half], to_z[-1]),
    ]]
    for step in (3, 2):
        for sign in (1, -1):
            j = m(z + sign * step, nz)
            zb[j] = input_block(j).astype(BF16)

    def z_step(step):
        pieces = ((top_half, low_half) if step == 3 else (pl.ds(0, length),) * 2)
        new = []
        for i, sign in ((0, 1), (1, -1)):
            j = m(z + sign * step, nz)
            zs[-1][i].wait_recv()
            piece = pieces[i]
            value = zb[j, piece].astype(F32) + zr[i, 3 - step, piece].astype(F32)
            zb[j, piece] = value.astype(BF16)
            new.append(send(zb.at[j], zr.at[i, 4 - step], to_z[sign]))
        zs.append(new)

    z_step(3)
    kv_copy.wait_recv()
    weight_part(1, True)
    rs_k.first()
    weight_part(2, False)
    rs_v.first()
    z_step(2)
    rs_q.third()
    for sign in (1, -1):
        j = m(z + sign, nz)
        zb[j] = input_block(j).astype(BF16)
    rs_k.second()
    rs_v.second()
    z_step(1)
    rs_q.fourth()
    rs_v.third()
    rs_k.third()
    last = input_block(z)
    rs_q.finish(dq_out)
    rs_v.fourth()
    rs_k.fourth()
    for copy in zs[-1]:
        copy.wait_recv()
    dx_out[...] = (last + zr[0, 3].astype(F32) + zr[1, 3].astype(F32)).astype(BF16)
    rs_v.finish(dv_out)
    rs_k.finish(dk_out)
    for copy in started:
        copy.wait_send()


def body(normed, queries, keys, values, grads, links, wq, wk, wv):
    length, cols = queries.shape[2:]
    width = normed.shape[-1]
    heads = cols // HD
    rows = wq.shape[0]
    vmem = pl.BlockSpec(memory_space=pltpu.VMEM)
    count = 96
    out = pl.pallas_call(
        kernel,
        out_shape=(
            jax.ShapeDtypeStruct((length, cols), BF16),
            jax.ShapeDtypeStruct((rows, cols), F32),
            jax.ShapeDtypeStruct((rows, cols), F32),
            jax.ShapeDtypeStruct((rows, cols), F32),
        ),
        in_specs=[pl.BlockSpec(memory_space=pltpu.SMEM)] + [vmem] * 8,
        out_specs=(vmem,) * 4,
        scratch_shapes=[
            pltpu.VMEM((2, 2, heads, length, HD), BF16),
            pltpu.VMEM((4, 2, 2, 2, rows, 3 * cols), BF16),
            pltpu.VMEM((4, 2, 2, 2, rows, length), BF16),
            pltpu.VMEM((4, 2, 2, rows, length), BF16),
            pltpu.VMEM((length, 3 * cols), BF16),
            pltpu.VMEM((length, 3 * cols), BF16),
            pltpu.VMEM((heads, 2, length, HD), F32),
            pltpu.VMEM((2, heads, 2, length, HD), BF16),
            pltpu.VMEM((2, heads, 2, length, HD), BF16),
            pltpu.VMEM((3, 4, 4, rows, cols), BF16),
            pltpu.VMEM((3, 2, 2, rows, cols), BF16),
            pltpu.VMEM((3, 2, 4, rows, cols), BF16),
            pltpu.VMEM((3, 4, rows, cols), BF16),
            pltpu.VMEM((3, 2, rows // 2, cols), BF16),
            pltpu.VMEM((3, 2, rows, cols), BF16),
            pltpu.VMEM((8, length, cols), BF16),
            pltpu.VMEM((2, 4, length, cols), BF16),
            pltpu.SemaphoreType.DMA((count,)),
            pltpu.SemaphoreType.DMA((count,)),
            pltpu.SemaphoreType.DMA((3,)),
        ],
        compiler_params=pltpu.CompilerParams(
            collective_id=0, has_side_effects=True, vmem_limit_bytes=56 * 1024 * 1024
        ),
        name="attention_backward",
    )(
        links,
        normed.reshape(length, width),
        *(value.reshape(length, cols) for value in (queries, keys, values, grads)),
        wq, wk, wv,
    )
    return (out[0].reshape(1, 1, length, cols), out[1], out[2], out[3])


def solution(mesh):
    tokens = P("dp", "view", None, "head")
    weight = P(("dp", "view"), "head")
    return jax.shard_map(
        body,
        mesh=mesh,
        in_specs=(P("dp", "view", None, None),) + (tokens,) * 4 + (P("view", None),) + (weight,) * 3,
        out_specs=(tokens,) + (weight,) * 3,
        check_vma=False,
    )
```

time: 596 us -> 109 us (0.18)
  the two profiles are of different devices: /device:TPU:1 before, /device:TPU:32 now
where the time goes in v1:
time: 109 us
  Pallas kernels  102 us (94%)
  local copies, waits for them, and re-layouts  6.36 us (6%)
    pallas_call x1, Pallas kernels, body(): pl.pallas_call(kernel, out_shape=(jax.ShapeDtypeStruct((length, cols), BF...  102 us
    unnamed x4, local copies, waits for them, and re-layouts  6.36 us

profile of v1, /device:TPU:32, one launch (start us, length us, event | category | flops | bytes accessed | tf_op | source)
XLA Modules:
  0.0 109.0 jit_solution(1670228685343035883)
XLA Ops:
  0.6 102.0 %attention_backward.1 = (bf16[256,384]{1,0:T(8,128)(2,1)}, f32[96,384]{1,0:T(8,128)}, f32[96,384]{1,0:T(8,128)}, f32[96,384]{1,0:T(8,128)}) custom-call(s32[1,2]{1,0:T(1,128)} %links.1, bf16[256,3072]{1,0:T(8,128)(2,1)} %bitcast.6, bf16[256,384]{1,0:T(8,128)(2,1)} %bitcast.7, bf16[256,384]{1,0:T(8,128)(2,1)} %bitcast.8, bf16[256,384]{1,0:T(8,128)(2,1)} %bitcast.9, ...), custom_call_target="tpu_custom_call" | custom-call | tf_op jit(solution)/shard_map/attention_backward/pallas_call | solution.py:351
  102.6 1.6 %copy.17 = bf16[1,1,256,384]{3,2,1,0:T(8,128)(2,1)} copy(bf16[1,1,256,384]{3,2,1,0:T(8,128)(2,1)} %bitcast.11) | data formatting | bytes 393216
  104.3 1.6 %copy.18 = f32[96,384]{1,0:T(8,128)} copy(f32[96,384]{1,0:T(8,128)} %get-tuple-element.17) | data formatting | bytes 294912
  105.9 1.6 %copy.19 = f32[96,384]{1,0:T(8,128)} copy(f32[96,384]{1,0:T(8,128)} %get-tuple-element.18) | data formatting | bytes 294912
  107.4 1.6 %copy.20 = f32[96,384]{1,0:T(8,128)} copy(f32[96,384]{1,0:T(8,128)} %get-tuple-element.19) | data formatting | bytes 294912

commit v2 on v1

--- a/solution.py
+++ b/solution.py
@@ -1,4 +1,4 @@
-import functools
+import contextlib
 
 import jax
 import jax.numpy as jnp
@@ -8,6 +8,7 @@
 from jax.sharding import PartitionSpec as P
 
 HD = 128
+SPLIT = 64
 MESH = pl.DeviceIdType.MESH
 F32 = jnp.float32
 BF16 = jnp.bfloat16
@@ -16,13 +17,18 @@
 TN = (((0,), (0,)), ((), ()))
 
 
+def scope(name):
+    return contextlib.nullcontext()
+
+
 def dot(a, b, dims):
     return lax.dot_general(a, b, dims, preferred_element_type=F32)
 
 
 def kernel(
-    links, normed, q_ref, k_ref, v_ref, g_ref, wq, wk, wv,
+    links, n_hbm, q_hbm, k_hbm, v_hbm, g_hbm, wq, wk, wv,
     dx_out, dq_out, dk_out, dv_out,
+    normed, q_ref, k_ref, v_ref, g_ref,
     kv, wg, nt, ntp, hown, hpar, own, gs, gr, part, ra1, rra, rb, rb1, rrb, zb, zr,
     ssem, rsem, lsem,
 ):
@@ -69,15 +75,84 @@
         for step in (1, -1):
             pl.semaphore_signal(barrier, inc=1, device_id=peers[step], device_id_type=MESH)
     yl = dp
-    locals_ = []
-    for i, w in enumerate((wq, wk, wv)):
-        copy = pltpu.make_async_copy(
-            w, wg.at[x, yl, yh, c, :, pl.ds(i * cols, cols)], lsem.at[i]
-        )
+
+    def load(src, dst, slot):
+        copy = pltpu.make_async_copy(src, dst, lsem.at[slot])
         copy.start()
-        locals_.append(copy)
-    pl.semaphore_wait(barrier, 8)
-
+        return copy
+
+    w_loads = [
+        load(w, wg.at[x, yl, yh, c, :, pl.ds(i * cols, cols)], i)
+        for i, w in enumerate((wq, wk, wv))
+    ]
+    kv_loads = [load(k_hbm, k_ref, 3), load(v_hbm, v_ref, 4)]
+    loads = [load(q_hbm, q_ref, 5), load(g_hbm, g_ref, 6), load(n_hbm, normed, 7)]
+    for copy in w_loads + kv_loads:
+        copy.wait()
+    with scope("barrier"):
+        pl.semaphore_wait(barrier, 8)
+
+    class Gather:
+        def __init__(self, start, size, x_first):
+            self.x_first = x_first
+            self.all = pl.ds(start, size)
+            self.lo, self.hi = pl.ds(start, size // 2), pl.ds(start + size // 2, size // 2)
+            self.to_a, self.to_b = (to_x, to_y) if x_first else (to_y, to_x)
+            self.b1, self.b2, self.par = {}, {}, []
+
+        def ref(self, ao, bo, piece):
+            xo, yo = (ao, bo) if self.x_first else (bo, ao)
+            yy = m(y + yo, 4)
+            return wg.at[m(x + xo, 4), lax.rem(yy, 2), lax.div(yy, 2), c, piece]
+
+        def pass_on(self, ao, bo, piece, device):
+            block = self.ref(ao, bo, piece)
+            return send(block, block, device)
+
+        def start(self):
+            self.a1 = [self.pass_on(0, 0, self.all, self.to_a[s]) for s in (1, -1)]
+
+        def across(self, ao):
+            self.b1[ao] = [self.pass_on(ao, 0, self.all, self.to_b[s]) for s in (1, -1)]
+
+        def forward(self):
+            for copy in self.a1:
+                copy.wait_recv()
+            self.a2 = [
+                self.pass_on(-1, 0, self.lo, self.to_a[1]),
+                self.pass_on(1, 0, self.hi, self.to_a[-1]),
+            ]
+
+        def far(self):
+            for copy in self.a2:
+                copy.wait_recv()
+
+        def across_forward(self, ao):
+            for copy in self.b1[ao]:
+                copy.wait_recv()
+            self.b2[ao] = [
+                self.pass_on(ao, -1, self.lo, self.to_b[1]),
+                self.pass_on(ao, 1, self.hi, self.to_b[-1]),
+            ]
+
+        def across_far(self):
+            for copies in self.b2.values():
+                for copy in copies:
+                    copy.wait_recv()
+
+        def to_partner(self, bo):
+            if self.x_first:
+                yy = m(y + bo, 4)
+                block = wg.at[:, lax.rem(yy, 2), lax.div(yy, 2), c, self.all]
+            else:
+                block = wg.at[m(x + bo, 4), :, :, c, self.all]
+            self.par.append(send(block, block, partner))
+
+    ga = Gather(0, SPLIT, False)
+    gb = Gather(SPLIT, rows - SPLIT, True)
+    ga.start()
+    gb.start()
+    ga.across(0)
     halo = []
     for h in range(heads):
         hs = pl.ds(h * HD, HD)
@@ -86,10 +161,10 @@
             copies.append(send(k_ref.at[:, hs], kv.at[slot, 0, h], to_view[step]))
             copies.append(send(v_ref.at[:, hs], kv.at[slot, 1, h], to_view[step]))
         halo.append(copies)
-    for copy in locals_:
+    gb.across(0)
+    for copy in loads:
         copy.wait()
-    mine = wg.at[x, yl, yh, c]
-    w_y1 = [send(mine, mine, to_y[s]) for s in (1, -1)]
+    lo, hi = pl.ds(0, half), pl.ds(half, half)
 
     def transpose_chunk(i, _):
         chunk = normed[:, pl.ds(pl.multiple_of(i * 4 * rows, 128), 4 * rows)]
@@ -97,21 +172,21 @@
         nt[lax.rem(i, 4), lax.div(i, 4)] = turned
         return 0
 
-    lax.fori_loop(0, 8, transpose_chunk, 0)
-
-    for copy in w_y1:
-        copy.wait_recv()
-    lo, hi = pl.ds(0, half), pl.ds(half, half)
-
-    def block_y(yy):
-        return lax.rem(yy, 2), lax.div(yy, 2)
-
-    a0, a1 = block_y(y_dn)
-    b0, b1 = block_y(y_up)
-    from_dn = wg.at[x, a0, a1, c, lo]
-    from_up = wg.at[x, b0, b1, c, hi]
-    w_y2 = [send(from_dn, from_dn, to_y[1]), send(from_up, from_up, to_y[-1])]
+    with scope("transpose"):
+        lax.fori_loop(0, 8, transpose_chunk, 0)
+    with scope("ga_forward"):
+        ga.forward()
+        ga.across(-1)
+        ga.across(1)
+    with scope("gb_forward"):
+        gb.forward()
     turned_copy = send(nt.at[:, :, :, 1 - c], ntp, partner)
+    with scope("ga_af0"):
+        ga.across_forward(0)
+    with scope("ga_far"):
+        ga.far()
+        ga.across(2)
+        ga.to_partner(0)
 
     pen = [
         jnp.where(links[0, 0] >= 0, 0.0, -1e30).astype(F32),
@@ -156,28 +231,26 @@
             ]
         )
 
-    attention(0)
-    for copy in w_y2:
-        copy.wait_recv()
-    column = wg.at[x, :, :, c]
-    w_x1 = [send(column, column, to_x[s]) for s in (1, -1)]
-    w_par.append(send(column, column, partner))
-    for h in range(1, heads):
-        attention(h)
-        if h == 1:
-            for copy in w_x1:
-                copy.wait_recv()
-            up, dn = wg.at[x_dn, 0, :, c], wg.at[x_up, 1, :, c]
-            w_x2 = [send(up, up, to_x[1]), send(dn, dn, to_x[-1])]
-            for xx in (x_dn, x_up):
-                column = wg.at[xx, :, :, c]
-                w_par.append(send(column, column, partner))
+    for h in range(heads):
+        with scope("att"):
+            attention(h)
     hq = hown.at[:, pl.ds(0, cols)]
     q_copy = send(hq, hpar.at[:, pl.ds(0, cols)], partner)
-    for copy in w_x2:
-        copy.wait_recv()
-    column = wg.at[x_far, :, :, c]
-    w_par.append(send(column, column, partner))
+    with scope("gb_far"):
+        gb.across(-1)
+        gb.across(1)
+        gb.far()
+        gb.across(2)
+        gb.to_partner(0)
+    with scope("ga_af1"):
+        ga.across_forward(-1)
+        ga.across_forward(1)
+    with scope("gb_af0"):
+        gb.across_forward(0)
+    with scope("ga_af2"):
+        ga.across_forward(2)
+        ga.to_partner(-1)
+        ga.to_partner(1)
 
     def weight_part(ci, x_first):
         cs = slice(ci * cols, (ci + 1) * cols)
@@ -261,84 +334,129 @@
             value = rb[ci, self.pb].astype(F32) + rrb[ci, 0].astype(F32)
             out[...] = (value + rrb[ci, 1].astype(F32)) * (1.0 / 32.0)
 
-    rs_q = Scatter(0, x, to_x, y, to_y)
+    rs_q = Scatter(0, y, to_y, x, to_x)
     rs_k = Scatter(1, x, to_x, y, to_y)
     rs_v = Scatter(2, y, to_y, x, to_x)
 
-    turned_copy.wait_recv()
-    q_copy.wait_recv()
-    weight_part(0, True)
+    with scope("wp_q"):
+        turned_copy.wait_recv()
+        q_copy.wait_recv()
+        weight_part(0, False)
+    with scope("gb_af1"):
+        gb.across_forward(-1)
+        gb.across_forward(1)
+    with scope("gb_af2"):
+        gb.across_forward(2)
+        gb.to_partner(-1)
+        gb.to_partner(1)
     rs_q.first()
-
-    for h in range(heads):
-        for copy in grad_halo[h]:
-            copy.wait_recv()
-        for i in range(2):
-            value = own[h, i] + gr[0, h, i].astype(F32) + gr[1, h, i].astype(F32)
-            start = (1 + i) * cols + h * HD
-            hown[:, start : start + HD] = value.astype(BF16)
+    with scope("gh_wait"):
+        for h in range(heads):
+            for copy in grad_halo[h]:
+                copy.wait_recv()
+            for i in range(2):
+                value = own[h, i] + gr[0, h, i].astype(F32) + gr[1, h, i].astype(F32)
+                start = (1 + i) * cols + h * HD
+                hown[:, start : start + HD] = value.astype(BF16)
     hkv = pl.ds(cols, 2 * cols)
     kv_copy = send(hown.at[:, hkv], hpar.at[:, hkv], partner)
-    rs_q.second()
-    for copy in w_par:
-        copy.wait_recv()
+    with scope("ga_bf"):
+        ga.across_far()
+        ga.to_partner(2)
+    with scope("gb_bf"):
+        gb.across_far()
+        gb.to_partner(2)
+    with scope("wpar"):
+        for copy in ga.par + gb.par:
+            copy.wait_recv()
 
     def input_block(j):
         w = wg[lax.rem(j, 4), lax.div(j, 4)].reshape(4 * rows, 3 * cols)
         return dot(hown[...], w, NT)
 
-    top_half, low_half = pl.ds(0, length // 2), pl.ds(length // 2, length // 2)
+    part_rows = length // 2
+    half_rows = part_rows // 2
     far = m(z + 4, nz)
-    zb[far] = input_block(far).astype(BF16)
-    zs = [[
-        send(zb.at[far, top_half], zr.at[0, 0, top_half], to_z[1]),
-        send(zb.at[far, low_half], zr.at[1, 0, low_half], to_z[-1]),
-    ]]
-    for step in (3, 2):
-        for sign in (1, -1):
-            j = m(z + sign * step, nz)
-            zb[j] = input_block(j).astype(BF16)
-
-    def z_step(step):
-        pieces = ((top_half, low_half) if step == 3 else (pl.ds(0, length),) * 2)
-        new = []
+    with scope("zfar"):
+        zb[far] = input_block(far).astype(BF16)
+    zs = [[], []]
+    for p in range(2):
         for i, sign in ((0, 1), (1, -1)):
-            j = m(z + sign * step, nz)
-            zs[-1][i].wait_recv()
-            piece = pieces[i]
-            value = zb[j, piece].astype(F32) + zr[i, 3 - step, piece].astype(F32)
-            zb[j, piece] = value.astype(BF16)
-            new.append(send(zb.at[j], zr.at[i, 4 - step], to_z[sign]))
-        zs.append(new)
-
-    z_step(3)
-    kv_copy.wait_recv()
-    weight_part(1, True)
+            piece = pl.ds(p * part_rows + i * half_rows, half_rows)
+            zs[p].append(send(zb.at[far, piece], zr.at[i, 0, piece], to_z[sign]))
+
+    def z_block(step):
+        with scope("zb"):
+            for sign in (1, -1):
+                j = m(z + sign * step, nz)
+                zb[j] = input_block(j).astype(BF16)
+
+    def z_step(step, p):
+        with scope("z%d%d" % (step, p)):
+            new = []
+            whole = pl.ds(p * part_rows, part_rows)
+            for i, sign in ((0, 1), (1, -1)):
+                piece = pl.ds(p * part_rows + i * half_rows, half_rows) if step == 3 else whole
+                j = m(z + sign * step, nz)
+                zs[p][i].wait_recv()
+                value = zb[j, piece].astype(F32) + zr[i, 3 - step, piece].astype(F32)
+                zb[j, piece] = value.astype(BF16)
+                new.append(send(zb.at[j, whole], zr.at[i, 4 - step, whole], to_z[sign]))
+            zs[p] = new
+
+    z_block(3)
+    z_block(2)
+    with scope("wp_k"):
+        kv_copy.wait_recv()
+        weight_part(1, True)
     rs_k.first()
-    weight_part(2, False)
+    z_step(3, 0)
+    z_step(3, 1)
+    with scope("wp_v"):
+        weight_part(2, False)
     rs_v.first()
-    z_step(2)
-    rs_q.third()
-    for sign in (1, -1):
-        j = m(z + sign, nz)
-        zb[j] = input_block(j).astype(BF16)
-    rs_k.second()
-    rs_v.second()
-    z_step(1)
-    rs_q.fourth()
-    rs_v.third()
-    rs_k.third()
+    with scope("q2"):
+        rs_q.second()
+    z_step(2, 0)
+    z_step(2, 1)
+    z_block(1)
+    with scope("k2"):
+        rs_k.second()
+    with scope("q3"):
+        rs_q.third()
+    with scope("v2"):
+        rs_v.second()
+    z_step(1, 0)
+    z_step(1, 1)
+    with scope("k3"):
+        rs_k.third()
+    with scope("q4"):
+        rs_q.fourth()
+    with scope("v3"):
+        rs_v.third()
     last = input_block(z)
-    rs_q.finish(dq_out)
-    rs_v.fourth()
-    rs_k.fourth()
-    for copy in zs[-1]:
-        copy.wait_recv()
-    dx_out[...] = (last + zr[0, 3].astype(F32) + zr[1, 3].astype(F32)).astype(BF16)
-    rs_v.finish(dv_out)
-    rs_k.finish(dk_out)
+    with scope("k4"):
+        rs_k.fourth()
+    with scope("v4"):
+        rs_v.fourth()
+    with scope("q5"):
+        rs_q.finish(dq_out)
+    with scope("zlast"):
+        for copies in zs:
+            for copy in copies:
+                copy.wait_recv()
+        dx_out[...] = (last + zr[0, 3].astype(F32) + zr[1, 3].astype(F32)).astype(BF16)
+    with scope("k5"):
+        rs_k.finish(dk_out)
+    with scope("v5"):
+        rs_v.finish(dv_out)
     for copy in started:
         copy.wait_send()
+
+
+def publish(a, b, c, d, oa, ob, oc, od):
+    for src, dst in ((a, oa), (b, ob), (c, oc), (d, od)):
+        dst[...] = src[...]
 
 
 def body(normed, queries, keys, values, grads, links, wq, wk, wv):
@@ -347,7 +465,8 @@
     heads = cols // HD
     rows = wq.shape[0]
     vmem = pl.BlockSpec(memory_space=pltpu.VMEM)
-    count = 96
+    anywhere = pl.BlockSpec(memory_space=pl.ANY)
+    count = 144
     out = pl.pallas_call(
         kernel,
         out_shape=(
@@ -356,9 +475,11 @@
             jax.ShapeDtypeStruct((rows, cols), F32),
             jax.ShapeDtypeStruct((rows, cols), F32),
         ),
-        in_specs=[pl.BlockSpec(memory_space=pltpu.SMEM)] + [vmem] * 8,
+        in_specs=[pl.BlockSpec(memory_space=pltpu.SMEM)] + [anywhere] * 8,
         out_specs=(vmem,) * 4,
         scratch_shapes=[
+            pltpu.VMEM((length, width), BF16),
+            *[pltpu.VMEM((length, cols), BF16)] * 4,
             pltpu.VMEM((2, 2, heads, length, HD), BF16),
             pltpu.VMEM((4, 2, 2, 2, rows, 3 * cols), BF16),
             pltpu.VMEM((4, 2, 2, 2, rows, length), BF16),
@@ -378,7 +499,7 @@
             pltpu.VMEM((2, 4, length, cols), BF16),
             pltpu.SemaphoreType.DMA((count,)),
             pltpu.SemaphoreType.DMA((count,)),
-            pltpu.SemaphoreType.DMA((3,)),
+            pltpu.SemaphoreType.DMA((8,)),
         ],
         compiler_params=pltpu.CompilerParams(
             collective_id=0, has_side_effects=True, vmem_limit_bytes=56 * 1024 * 1024
@@ -390,6 +511,13 @@
         *(value.reshape(length, cols) for value in (queries, keys, values, grads)),
         wq, wk, wv,
     )
+    out = pl.pallas_call(
+        publish,
+        out_shape=[jax.ShapeDtypeStruct(o.shape, o.dtype) for o in out],
+        in_specs=[vmem] * 4,
+        out_specs=[vmem] * 4,
+        name="publish",
+    )(*out)
     return (out[0].reshape(1, 1, length, cols), out[1], out[2], out[3])
 
 

time: 109 us -> 85.7 us (0.79)
  the two profiles are of different devices: /device:TPU:32 before, /device:TPU:1 now
where the time goes in v2:
time: 85.7 us; the launch traced here: 84.6 us
  Pallas kernels  83.9 us (98%)
    pallas_call x1, Pallas kernels, body(): pl.pallas_call(kernel, out_shape=(jax.ShapeDtypeStruct((length, cols), BF...  82 us
    pallas_call x1, Pallas kernels, body(): pl.pallas_call(publish, out_shape=[jax.ShapeDtypeStruct(o.shape, o.dtype)...  1.98 us

profile of v2, /device:TPU:1, one launch (start us, length us, event | category | flops | bytes accessed | tf_op | source)
XLA Modules:
  0.0 84.6 jit_solution(10527712078415811378)
XLA Ops:
  0.6 82.0 %attention_backward.1 = (bf16[256,384]{1,0:T(8,128)(2,1)}, f32[96,384]{1,0:T(8,128)}, f32[96,384]{1,0:T(8,128)}, f32[96,384]{1,0:T(8,128)}) custom-call(s32[1,2]{1,0:T(1,128)} %links.1, bf16[256,3072]{1,0:T(8,128)(2,1)} %bitcast.6, bf16[256,384]{1,0:T(8,128)(2,1)} %bitcast.7, bf16[256,384]{1,0:T(8,128)(2,1)} %bitcast.8, bf16[256,384]{1,0:T(8,128)(2,1)} %bitcast.9, ...), custom_call_target="tpu_custom_call" | custom-call | tf_op jit(solution)/shard_map/attention_backward/pallas_call | solution.py:470
  82.6 2.0 %publish.1 = (bf16[256,384]{1,0:T(8,128)(2,1)}, f32[96,384]{1,0:T(8,128)}, f32[96,384]{1,0:T(8,128)}, f32[96,384]{1,0:T(8,128)}) custom-call(bf16[256,384]{1,0:T(8,128)(2,1)} %get-tuple-element.12.a, f32[96,384]{1,0:T(8,128)} %get-tuple-element.13.b, f32[96,384]{1,0:T(8,128)} %get-tuple-element.14.c, f32[96,384]{1,0:T(8,128)} %get-tuple-element.15.d), custom_call_target="tpu_custom_call" | custom-call | tf_op jit(solution)/shard_map/publish/pallas_call | solution.py:514

commit v3 on v2

--- a/solution.py
+++ b/solution.py
@@ -8,7 +8,6 @@
 from jax.sharding import PartitionSpec as P
 
 HD = 128
-SPLIT = 64
 MESH = pl.DeviceIdType.MESH
 F32 = jnp.float32
 BF16 = jnp.bfloat16
@@ -130,15 +129,19 @@
         def across_forward(self, ao):
             for copy in self.b1[ao]:
                 copy.wait_recv()
+            third = rows // 3
+            turn = 1 - 2 * yh
+            turn_to = at(m(x + turn, 4), y, c, z)
             self.b2[ao] = [
-                self.pass_on(ao, -1, self.lo, self.to_b[1]),
-                self.pass_on(ao, 1, self.hi, self.to_b[-1]),
-            ]
-
-        def across_far(self):
-            for copies in self.b2.values():
-                for copy in copies:
-                    copy.wait_recv()
+                self.pass_on(ao, -1, pl.ds(0, third), to_x[1]),
+                self.pass_on(ao, 1, pl.ds(2 * third, third), to_x[-1]),
+                self.pass_on(ao, -turn, pl.ds(third, third), turn_to),
+            ]
+
+        def across_far(self, ao):
+            for copy in self.b2[ao]:
+                copy.wait_recv()
+            self.par.append(self.pass_on(ao, 2, self.all, partner))
 
         def to_partner(self, bo):
             if self.x_first:
@@ -148,11 +151,9 @@
                 block = wg.at[m(x + bo, 4), :, :, c, self.all]
             self.par.append(send(block, block, partner))
 
-    ga = Gather(0, SPLIT, False)
-    gb = Gather(SPLIT, rows - SPLIT, True)
-    ga.start()
-    gb.start()
-    ga.across(0)
+    gather = Gather(0, rows, False)
+    gather.start()
+    gather.across(0)
     halo = []
     for h in range(heads):
         hs = pl.ds(h * HD, HD)
@@ -161,7 +162,6 @@
             copies.append(send(k_ref.at[:, hs], kv.at[slot, 0, h], to_view[step]))
             copies.append(send(v_ref.at[:, hs], kv.at[slot, 1, h], to_view[step]))
         halo.append(copies)
-    gb.across(0)
     for copy in loads:
         copy.wait()
     lo, hi = pl.ds(0, half), pl.ds(half, half)
@@ -175,18 +175,12 @@
     with scope("transpose"):
         lax.fori_loop(0, 8, transpose_chunk, 0)
     with scope("ga_forward"):
-        ga.forward()
-        ga.across(-1)
-        ga.across(1)
-    with scope("gb_forward"):
-        gb.forward()
+        gather.forward()
+        gather.across(-1)
+        gather.across(1)
     turned_copy = send(nt.at[:, :, :, 1 - c], ntp, partner)
     with scope("ga_af0"):
-        ga.across_forward(0)
-    with scope("ga_far"):
-        ga.far()
-        ga.across(2)
-        ga.to_partner(0)
+        gather.across_forward(0)
 
     pen = [
         jnp.where(links[0, 0] >= 0, 0.0, -1e30).astype(F32),
@@ -236,21 +230,13 @@
             attention(h)
     hq = hown.at[:, pl.ds(0, cols)]
     q_copy = send(hq, hpar.at[:, pl.ds(0, cols)], partner)
-    with scope("gb_far"):
-        gb.across(-1)
-        gb.across(1)
-        gb.far()
-        gb.across(2)
-        gb.to_partner(0)
+    with scope("ga_far"):
+        gather.far()
+        gather.across(2)
+        gather.to_partner(0)
     with scope("ga_af1"):
-        ga.across_forward(-1)
-        ga.across_forward(1)
-    with scope("gb_af0"):
-        gb.across_forward(0)
-    with scope("ga_af2"):
-        ga.across_forward(2)
-        ga.to_partner(-1)
-        ga.to_partner(1)
+        gather.across_forward(-1)
+        gather.across_forward(1)
 
     def weight_part(ci, x_first):
         cs = slice(ci * cols, (ci + 1) * cols)
@@ -342,13 +328,6 @@
         turned_copy.wait_recv()
         q_copy.wait_recv()
         weight_part(0, False)
-    with scope("gb_af1"):
-        gb.across_forward(-1)
-        gb.across_forward(1)
-    with scope("gb_af2"):
-        gb.across_forward(2)
-        gb.to_partner(-1)
-        gb.to_partner(1)
     rs_q.first()
     with scope("gh_wait"):
         for h in range(heads):
@@ -360,14 +339,24 @@
                 hown[:, start : start + HD] = value.astype(BF16)
     hkv = pl.ds(cols, 2 * cols)
     kv_copy = send(hown.at[:, hkv], hpar.at[:, hkv], partner)
+    with scope("ga_af2"):
+        gather.across_forward(2)
+        gather.to_partner(-1)
+        gather.to_partner(1)
+    with scope("q2"):
+        rs_q.second()
+    with scope("wp_v"):
+        kv_copy.wait_recv()
+        weight_part(2, False)
+    rs_v.first()
+    with scope("wp_k"):
+        weight_part(1, True)
+    rs_k.first()
     with scope("ga_bf"):
-        ga.across_far()
-        ga.to_partner(2)
-    with scope("gb_bf"):
-        gb.across_far()
-        gb.to_partner(2)
+        for ao in (0, -1, 1, 2):
+            gather.across_far(ao)
     with scope("wpar"):
-        for copy in ga.par + gb.par:
+        for copy in gather.par:
             copy.wait_recv()
 
     def input_block(j):
@@ -405,51 +394,42 @@
             zs[p] = new
 
     z_block(3)
+    with scope("q3"):
+        rs_q.third()
     z_block(2)
-    with scope("wp_k"):
-        kv_copy.wait_recv()
-        weight_part(1, True)
-    rs_k.first()
+    with scope("v2"):
+        rs_v.second()
     z_step(3, 0)
     z_step(3, 1)
-    with scope("wp_v"):
-        weight_part(2, False)
-    rs_v.first()
-    with scope("q2"):
-        rs_q.second()
+    with scope("k2"):
+        rs_k.second()
+    z_block(1)
+    with scope("q4"):
+        rs_q.fourth()
     z_step(2, 0)
     z_step(2, 1)
-    z_block(1)
-    with scope("k2"):
-        rs_k.second()
-    with scope("q3"):
-        rs_q.third()
-    with scope("v2"):
-        rs_v.second()
+    with scope("v3"):
+        rs_v.third()
+    with scope("k3"):
+        rs_k.third()
+    last = input_block(z)
     z_step(1, 0)
     z_step(1, 1)
-    with scope("k3"):
-        rs_k.third()
-    with scope("q4"):
-        rs_q.fourth()
-    with scope("v3"):
-        rs_v.third()
-    last = input_block(z)
+    with scope("v4"):
+        rs_v.fourth()
     with scope("k4"):
         rs_k.fourth()
-    with scope("v4"):
-        rs_v.fourth()
     with scope("q5"):
         rs_q.finish(dq_out)
+    with scope("v5"):
+        rs_v.finish(dv_out)
+    with scope("k5"):
+        rs_k.finish(dk_out)
     with scope("zlast"):
         for copies in zs:
             for copy in copies:
                 copy.wait_recv()
         dx_out[...] = (last + zr[0, 3].astype(F32) + zr[1, 3].astype(F32)).astype(BF16)
-    with scope("k5"):
-        rs_k.finish(dk_out)
-    with scope("v5"):
-        rs_v.finish(dv_out)
     for copy in started:
         copy.wait_send()
 

time: 85.7 us -> 78.5 us (0.916); the launches traced: 84.6 us -> 78.3 us
  Pallas kernels: 83.9 us -> 77.7 us
    pallas_call x1, Pallas kernels: 82 us -> 75.7 us  [body(): pl.pallas_call(kernel, out_shape=(jax.ShapeDtypeStruct((length, cols), BF...]
where the time goes in v3:
time: 78.5 us; the launch traced here: 78.3 us
  Pallas kernels  77.7 us (99%)
    pallas_call x1, Pallas kernels, body(): pl.pallas_call(kernel, out_shape=(jax.ShapeDtypeStruct((length, cols), BF...  75.7 us
    pallas_call x1, Pallas kernels, body(): pl.pallas_call(publish, out_shape=[jax.ShapeDtypeStruct(o.shape, o.dtype)...  1.98 us

profile of v3, /device:TPU:1, one launch (start us, length us, event | category | flops | bytes accessed | tf_op | source)
XLA Modules:
  0.0 78.3 jit_solution(11271877353011060539)
XLA Ops:
  0.6 75.7 %attention_backward.1 = (bf16[256,384]{1,0:T(8,128)(2,1)}, f32[96,384]{1,0:T(8,128)}, f32[96,384]{1,0:T(8,128)}, f32[96,384]{1,0:T(8,128)}) custom-call(s32[1,2]{1,0:T(1,128)} %links.1, bf16[256,3072]{1,0:T(8,128)(2,1)} %bitcast.6, bf16[256,384]{1,0:T(8,128)(2,1)} %bitcast.7, bf16[256,384]{1,0:T(8,128)(2,1)} %bitcast.8, bf16[256,384]{1,0:T(8,128)(2,1)} %bitcast.9, ...), custom_call_target="tpu_custom_call" | custom-call | tf_op jit(solution)/shard_map/attention_backward/pallas_call | solution.py:450
  76.3 2.0 %publish.1 = (bf16[256,384]{1,0:T(8,128)(2,1)}, f32[96,384]{1,0:T(8,128)}, f32[96,384]{1,0:T(8,128)}, f32[96,384]{1,0:T(8,128)}) custom-call(bf16[256,384]{1,0:T(8,128)(2,1)} %get-tuple-element.12.a, f32[96,384]{1,0:T(8,128)} %get-tuple-element.13.b, f32[96,384]{1,0:T(8,128)} %get-tuple-element.14.c, f32[96,384]{1,0:T(8,128)} %get-tuple-element.15.d), custom_call_target="tpu_custom_call" | custom-call | tf_op jit(solution)/shard_map/publish/pallas_call | solution.py:494

commit v4 on v3

--- a/solution.py
+++ b/solution.py
@@ -8,6 +8,7 @@
 from jax.sharding import PartitionSpec as P
 
 HD = 128
+SPLIT = 64
 MESH = pl.DeviceIdType.MESH
 F32 = jnp.float32
 BF16 = jnp.bfloat16
@@ -47,7 +48,7 @@
         return (lax.rem(yy, 2), xx * 4 + lax.div(yy, 2) * 2 + cc, zz)
 
     def m(value, n):
-        return lax.rem(value + n, n)
+        return lax.rem(value + 2 * n, n)
 
     x_up, x_dn, x_far = m(x + 1, 4), m(x - 1, 4), m(x + 2, 4)
     y_up, y_dn = m(y + 1, 4), m(y - 1, 4)
@@ -91,13 +92,19 @@
     with scope("barrier"):
         pl.semaphore_wait(barrier, 8)
 
+    turn = 1 - 2 * yh
+    to_turn = at(m(x + turn, 4), y, c, z)
+
     class Gather:
         def __init__(self, start, size, x_first):
             self.x_first = x_first
             self.all = pl.ds(start, size)
-            self.lo, self.hi = pl.ds(start, size // 2), pl.ds(start + size // 2, size // 2)
             self.to_a, self.to_b = (to_x, to_y) if x_first else (to_y, to_x)
-            self.b1, self.b2, self.par = {}, {}, []
+            self.half = (pl.ds(start, size // 2), pl.ds(start + size // 2, size // 2))
+            side = size // 4
+            self.outer = (pl.ds(start, side), pl.ds(start + size - side, side))
+            self.inner = pl.ds(start + side, size - 2 * side)
+            self.b1, self.b2, self.par, self.tail = {}, {}, {}, []
 
         def ref(self, ao, bo, piece):
             xo, yo = (ao, bo) if self.x_first else (bo, ao)
@@ -117,10 +124,10 @@
         def forward(self):
             for copy in self.a1:
                 copy.wait_recv()
-            self.a2 = [
-                self.pass_on(-1, 0, self.lo, self.to_a[1]),
-                self.pass_on(1, 0, self.hi, self.to_a[-1]),
-            ]
+            if self.x_first:
+                self.a2 = [self.pass_on(-turn, 0, self.all, to_turn)]
+            else:
+                self.a2 = [self.pass_on(-s, 0, self.half[i], self.to_a[s]) for i, s in enumerate((1, -1))]
 
         def far(self):
             for copy in self.a2:
@@ -129,19 +136,16 @@
         def across_forward(self, ao):
             for copy in self.b1[ao]:
                 copy.wait_recv()
-            third = rows // 3
-            turn = 1 - 2 * yh
-            turn_to = at(m(x + turn, 4), y, c, z)
-            self.b2[ao] = [
-                self.pass_on(ao, -1, pl.ds(0, third), to_x[1]),
-                self.pass_on(ao, 1, pl.ds(2 * third, third), to_x[-1]),
-                self.pass_on(ao, -turn, pl.ds(third, third), turn_to),
-            ]
+            if self.x_first:
+                self.b2[ao] = [self.pass_on(ao, -s, self.half[i], self.to_b[s]) for i, s in enumerate((1, -1))]
+            else:
+                self.b2[ao] = [self.pass_on(ao, -s, self.outer[i], self.to_b[s]) for i, s in enumerate((1, -1))]
+                self.b2[ao].append(self.pass_on(ao, -turn, self.inner, to_turn))
 
         def across_far(self, ao):
             for copy in self.b2[ao]:
                 copy.wait_recv()
-            self.par.append(self.pass_on(ao, 2, self.all, partner))
+            self.tail.append(self.pass_on(ao, 2, self.all, partner))
 
         def to_partner(self, bo):
             if self.x_first:
@@ -149,11 +153,13 @@
                 block = wg.at[:, lax.rem(yy, 2), lax.div(yy, 2), c, self.all]
             else:
                 block = wg.at[m(x + bo, 4), :, :, c, self.all]
-            self.par.append(send(block, block, partner))
-
-    gather = Gather(0, rows, False)
-    gather.start()
-    gather.across(0)
+            self.par[bo] = send(block, block, partner)
+
+    ga = Gather(0, SPLIT, False)
+    gb = Gather(SPLIT, rows - SPLIT, True)
+    ga.start()
+    gb.start()
+    ga.across(0)
     halo = []
     for h in range(heads):
         hs = pl.ds(h * HD, HD)
@@ -162,6 +168,7 @@
             copies.append(send(k_ref.at[:, hs], kv.at[slot, 0, h], to_view[step]))
             copies.append(send(v_ref.at[:, hs], kv.at[slot, 1, h], to_view[step]))
         halo.append(copies)
+    gb.across(0)
     for copy in loads:
         copy.wait()
     lo, hi = pl.ds(0, half), pl.ds(half, half)
@@ -174,13 +181,17 @@
 
     with scope("transpose"):
         lax.fori_loop(0, 8, transpose_chunk, 0)
+    with scope("gb_forward"):
+        gb.forward()
     with scope("ga_forward"):
-        gather.forward()
-        gather.across(-1)
-        gather.across(1)
+        ga.forward()
+        ga.across(-1)
+        ga.across(1)
+    gb.across(-1)
+    gb.across(1)
     turned_copy = send(nt.at[:, :, :, 1 - c], ntp, partner)
     with scope("ga_af0"):
-        gather.across_forward(0)
+        ga.across_forward(0)
 
     pen = [
         jnp.where(links[0, 0] >= 0, 0.0, -1e30).astype(F32),
@@ -231,25 +242,28 @@
     hq = hown.at[:, pl.ds(0, cols)]
     q_copy = send(hq, hpar.at[:, pl.ds(0, cols)], partner)
     with scope("ga_far"):
-        gather.far()
-        gather.across(2)
-        gather.to_partner(0)
+        ga.far()
+        ga.across(2)
+        ga.to_partner(0)
+    with scope("gb_far"):
+        gb.far()
+        gb.across(2)
+        gb.to_partner(0)
     with scope("ga_af1"):
-        gather.across_forward(-1)
-        gather.across_forward(1)
-
+        ga.across_forward(-1)
+        ga.across_forward(1)
     def weight_part(ci, x_first):
         cs = slice(ci * cols, (ci + 1) * cols)
 
         def step(xx, _):
+            a = nt[xx, :, :, c].reshape(4 * rows, length)
+            b = ntp[xx].reshape(4 * rows, length)
+            acc = dot(a, hown[:, cs], NN) + dot(b, hpar[:, cs], NN)
+            acc = acc.astype(BF16)
             for ll in range(2):
-                a = jnp.concatenate([nt[xx, ll, 0, c], nt[xx, ll, 1, c]], axis=0)
-                b = ntp[xx, ll].reshape(2 * rows, length)
-                acc = dot(a, hown[:, cs], NN) + dot(b, hpar[:, cs], NN)
-                acc = acc.astype(BF16)
                 for hh in range(2):
-                    yy = hh * 2 + ll
-                    block = acc[hh * rows : (hh + 1) * rows]
+                    yy, start = hh * 2 + ll, (ll * 2 + hh) * rows
+                    block = acc[start : start + rows]
                     if x_first:
                         part[ci, xx, yy] = block
                     else:
@@ -320,15 +334,25 @@
             value = rb[ci, self.pb].astype(F32) + rrb[ci, 0].astype(F32)
             out[...] = (value + rrb[ci, 1].astype(F32)) * (1.0 / 32.0)
 
-    rs_q = Scatter(0, y, to_y, x, to_x)
+    rs_q = Scatter(0, x, to_x, y, to_y)
     rs_k = Scatter(1, x, to_x, y, to_y)
     rs_v = Scatter(2, y, to_y, x, to_x)
 
     with scope("wp_q"):
         turned_copy.wait_recv()
         q_copy.wait_recv()
-        weight_part(0, False)
+        weight_part(0, True)
+    with scope("ga_af2"):
+        ga.across_forward(2)
+        ga.to_partner(-1)
+        ga.to_partner(1)
     rs_q.first()
+    with scope("ga_bf0"):
+        ga.across_far(0)
+    with scope("gb_af1"):
+        gb.across_forward(0)
+        gb.across_forward(-1)
+        gb.across_forward(1)
     with scope("gh_wait"):
         for h in range(heads):
             for copy in grad_halo[h]:
@@ -339,25 +363,26 @@
                 hown[:, start : start + HD] = value.astype(BF16)
     hkv = pl.ds(cols, 2 * cols)
     kv_copy = send(hown.at[:, hkv], hpar.at[:, hkv], partner)
-    with scope("ga_af2"):
-        gather.across_forward(2)
-        gather.to_partner(-1)
-        gather.to_partner(1)
-    with scope("q2"):
-        rs_q.second()
+    with scope("gb_af2"):
+        gb.across_forward(2)
+        gb.to_partner(-1)
+        gb.to_partner(1)
+    with scope("ga_bf1"):
+        ga.across_far(-1)
+        ga.across_far(1)
     with scope("wp_v"):
         kv_copy.wait_recv()
         weight_part(2, False)
     rs_v.first()
-    with scope("wp_k"):
-        weight_part(1, True)
-    rs_k.first()
     with scope("ga_bf"):
+        ga.across_far(2)
+    with scope("gb_bf"):
         for ao in (0, -1, 1, 2):
-            gather.across_far(ao)
+            gb.across_far(ao)
     with scope("wpar"):
-        for copy in gather.par:
-            copy.wait_recv()
+        for group in (ga, gb):
+            for copy in list(group.par.values()) + group.tail:
+                copy.wait_recv()
 
     def input_block(j):
         w = wg[lax.rem(j, 4), lax.div(j, 4)].reshape(4 * rows, 3 * cols)
@@ -393,28 +418,33 @@
                 new.append(send(zb.at[j, whole], zr.at[i, 4 - step, whole], to_z[sign]))
             zs[p] = new
 
+    with scope("wp_k"):
+        weight_part(1, True)
+    with scope("q2"):
+        rs_q.second()
+    rs_k.first()
     z_block(3)
+    z_step(3, 0)
+    z_step(3, 1)
+    with scope("v2"):
+        rs_v.second()
+    z_block(2)
     with scope("q3"):
         rs_q.third()
-    z_block(2)
-    with scope("v2"):
-        rs_v.second()
-    z_step(3, 0)
-    z_step(3, 1)
+    z_step(2, 0)
+    z_step(2, 1)
     with scope("k2"):
         rs_k.second()
     z_block(1)
+    with scope("v3"):
+        rs_v.third()
+    z_step(1, 0)
     with scope("q4"):
         rs_q.fourth()
-    z_step(2, 0)
-    z_step(2, 1)
-    with scope("v3"):
-        rs_v.third()
+    z_step(1, 1)
+    last = input_block(z)
     with scope("k3"):
         rs_k.third()
-    last = input_block(z)
-    z_step(1, 0)
-    z_step(1, 1)
     with scope("v4"):
         rs_v.fourth()
     with scope("k4"):
@@ -423,13 +453,13 @@
         rs_q.finish(dq_out)
     with scope("v5"):
         rs_v.finish(dv_out)
-    with scope("k5"):
-        rs_k.finish(dk_out)
     with scope("zlast"):
         for copies in zs:
             for copy in copies:
                 copy.wait_recv()
         dx_out[...] = (last + zr[0, 3].astype(F32) + zr[1, 3].astype(F32)).astype(BF16)
+    with scope("k5"):
+        rs_k.finish(dk_out)
     for copy in started:
         copy.wait_send()
 
@@ -446,7 +476,7 @@
     rows = wq.shape[0]
     vmem = pl.BlockSpec(memory_space=pltpu.VMEM)
     anywhere = pl.BlockSpec(memory_space=pl.ANY)
-    count = 144
+    count = 176
     out = pl.pallas_call(
         kernel,
         out_shape=(

time: 78.5 us -> 75.2 us (0.958)
  Pallas kernels: 77.7 us -> 74.3 us
    pallas_call x1, Pallas kernels: 75.7 us -> 72.4 us  [body(): pl.pallas_call(kernel, out_shape=(jax.ShapeDtypeStruct((length, cols), BF...]
where the time goes in v4:
time: 75.2 us; the launch traced here: 75 us
  Pallas kernels  74.3 us (99%)
    pallas_call x1, Pallas kernels, body(): pl.pallas_call(kernel, out_shape=(jax.ShapeDtypeStruct((length, cols), BF...  72.4 us
    pallas_call x1, Pallas kernels, body(): pl.pallas_call(publish, out_shape=[jax.ShapeDtypeStruct(o.shape, o.dtype)...  1.98 us

profile of v4, /device:TPU:1, one launch (start us, length us, event | category | flops | bytes accessed | tf_op | source)
XLA Modules:
  0.0 75.0 jit_solution(14204602586328565929)
XLA Ops:
  0.6 72.4 %attention_backward.1 = (bf16[256,384]{1,0:T(8,128)(2,1)}, f32[96,384]{1,0:T(8,128)}, f32[96,384]{1,0:T(8,128)}, f32[96,384]{1,0:T(8,128)}) custom-call(s32[1,2]{1,0:T(1,128)} %links.1, bf16[256,3072]{1,0:T(8,128)(2,1)} %bitcast.6, bf16[256,384]{1,0:T(8,128)(2,1)} %bitcast.7, bf16[256,384]{1,0:T(8,128)(2,1)} %bitcast.8, bf16[256,384]{1,0:T(8,128)(2,1)} %bitcast.9, ...), custom_call_target="tpu_custom_call" | custom-call | tf_op jit(solution)/shard_map/attention_backward/pallas_call | solution.py:480
  73.0 2.0 %publish.1 = (bf16[256,384]{1,0:T(8,128)(2,1)}, f32[96,384]{1,0:T(8,128)}, f32[96,384]{1,0:T(8,128)}, f32[96,384]{1,0:T(8,128)}) custom-call(bf16[256,384]{1,0:T(8,128)(2,1)} %get-tuple-element.12.a, f32[96,384]{1,0:T(8,128)} %get-tuple-element.13.b, f32[96,384]{1,0:T(8,128)} %get-tuple-element.14.c, f32[96,384]{1,0:T(8,128)} %get-tuple-element.15.d), custom_call_target="tpu_custom_call" | custom-call | tf_op jit(solution)/shard_map/publish/pallas_call | solution.py:524

commit v5 on v4

--- a/solution.py
+++ b/solution.py
@@ -27,9 +27,10 @@
 
 def kernel(
     links, n_hbm, q_hbm, k_hbm, v_hbm, g_hbm, wq, wk, wv,
+    dx_hbm, dq_hbm, dk_hbm, dv_hbm,
     dx_out, dq_out, dk_out, dv_out,
     normed, q_ref, k_ref, v_ref, g_ref,
-    kv, wg, nt, ntp, hown, hpar, own, gs, gr, part, ra1, rra, rb, rb1, rrb, zb, zr,
+    relay, kv, wg, nt, ntp, hown, hpar, own, gs, gr, part, ra1, rra, rb, rrb, zb, zr,
     ssem, rsem, lsem,
 ):
     length, cols = q_ref.shape
@@ -38,7 +39,7 @@
     half = rows // 2
     scaling = HD ** (-0.5)
     dp, vw, z = lax.axis_index("dp"), lax.axis_index("view"), lax.axis_index("head")
-    nview, nz = 16, 8
+    nz = 8
     x = lax.div(vw, 4)
     yh = lax.rem(lax.div(vw, 2), 2)
     c = lax.rem(vw, 2)
@@ -55,8 +56,16 @@
     to_x = {1: at(x_up, y, c, z), -1: at(x_dn, y, c, z)}
     to_y = {1: at(x, y_up, c, z), -1: at(x, y_dn, c, z)}
     to_z = {1: (dp, vw, m(z + 1, nz)), -1: (dp, vw, m(z - 1, nz))}
-    to_view = {1: (dp, m(vw + 1, nview), z), -1: (dp, m(vw - 1, nview), z)}
     partner = at(x, y, 1 - c, z)
+
+    def cross(yy):
+        upper = lax.div(yy, 2)
+        return c * upper - (1 - c) * (1 - upper)
+
+    def outward(yy):
+        return at(m(x + cross(yy), 4), m(yy + 2, 4), 1 - c, z)
+
+    over = (outward(m(y - 1, 4)), outward(m(y + 1, 4)))
 
     started = []
 
@@ -71,15 +80,23 @@
         return copy
 
     barrier = pltpu.get_barrier_semaphore()
-    for peers in (to_view, to_x, to_y, to_z):
-        for step in (1, -1):
-            pl.semaphore_signal(barrier, inc=1, device_id=peers[step], device_id_type=MESH)
+    peers = [partner, at(x_far, y, c, z), at(x, m(y + 2, 4), c, z)]
+    for ring in (to_x, to_y, to_z):
+        peers += [ring[1], ring[-1]]
+    peers += [at(m(x + cross(y), 4), m(y + s, 4), 1 - c, z) for s in (1, -1)]
+    for peer in peers:
+        pl.semaphore_signal(barrier, inc=1, device_id=peer, device_id_type=MESH)
     yl = dp
 
     def load(src, dst, slot):
         copy = pltpu.make_async_copy(src, dst, lsem.at[slot])
         copy.start()
         return copy
+
+    stored = []
+
+    def put(src, dst, slot):
+        stored.append(load(src, dst, slot))
 
     w_loads = [
         load(w, wg.at[x, yl, yh, c, :, pl.ds(i * cols, cols)], i)
@@ -90,7 +107,7 @@
     for copy in w_loads + kv_loads:
         copy.wait()
     with scope("barrier"):
-        pl.semaphore_wait(barrier, 8)
+        pl.semaphore_wait(barrier, len(peers))
 
     turn = 1 - 2 * yh
     to_turn = at(m(x + turn, 4), y, c, z)
@@ -160,15 +177,12 @@
     ga.start()
     gb.start()
     ga.across(0)
-    halo = []
+    halo, hops = [], []
     for h in range(heads):
         hs = pl.ds(h * HD, HD)
-        copies = []
-        for slot, step in ((0, 1), (1, -1)):
-            copies.append(send(k_ref.at[:, hs], kv.at[slot, 0, h], to_view[step]))
-            copies.append(send(v_ref.at[:, hs], kv.at[slot, 1, h], to_view[step]))
-        halo.append(copies)
-    gb.across(0)
+        pair = (k_ref.at[:, hs], v_ref.at[:, hs])
+        halo.append([send(pair[i], kv.at[c, i, h], partner) for i in range(2)])
+        hops.append([send(pair[i], relay.at[0, i, h], to_y[s]) for i, s in enumerate((1, -1))])
     for copy in loads:
         copy.wait()
     lo, hi = pl.ds(0, half), pl.ds(half, half)
@@ -187,18 +201,28 @@
         ga.forward()
         ga.across(-1)
         ga.across(1)
+    for h in range(heads):
+        with scope("relay%d" % h):
+            for i in range(2):
+                hops[h][i].wait_recv()
+                halo[h].append(send(relay.at[0, i, h], kv.at[1 - c, i, h], over[i]))
+    gb.across(0)
     gb.across(-1)
     gb.across(1)
     turned_copy = send(nt.at[:, :, :, 1 - c], ntp, partner)
     with scope("ga_af0"):
         ga.across_forward(0)
+    with scope("ga_far"):
+        ga.far()
+        ga.across(2)
+        ga.to_partner(0)
 
     pen = [
         jnp.where(links[0, 0] >= 0, 0.0, -1e30).astype(F32),
         None,
         jnp.where(links[0, 1] >= 0, 0.0, -1e30).astype(F32),
     ]
-    grad_halo = []
+    grad_halo, grad_hops = [], []
     w_x1, w_x2, w_par = [], [], []
 
     def attention(h):
@@ -229,52 +253,57 @@
             gs[slot, h, 1] = dot(probs[j].astype(BF16), gh, TN).astype(BF16)
         own[h, 0] = dot(sg[1], qh, TN)
         own[h, 1] = dot(probs[1].astype(BF16), gh, TN)
-        grad_halo.append(
-            [
-                send(gs.at[0, h], gr.at[0, h], to_view[-1]),
-                send(gs.at[1, h], gr.at[1, h], to_view[1]),
-            ]
+        grad_halo.append([send(gs.at[1 - c, h], gr.at[0, h], partner)])
+        grad_hops.append(
+            [send(gs.at[c, h, i], relay.at[1, i, h], to_y[s]) for i, s in enumerate((1, -1))]
         )
+
+    def grad_relay(h):
+        with scope("gr%d" % h):
+            for i in range(2):
+                grad_hops[h][i].wait_recv()
+                grad_halo[h].append(send(relay.at[1, i, h], gr.at[1, h, i], over[i]))
 
     for h in range(heads):
         with scope("att"):
             attention(h)
     hq = hown.at[:, pl.ds(0, cols)]
     q_copy = send(hq, hpar.at[:, pl.ds(0, cols)], partner)
-    with scope("ga_far"):
-        ga.far()
-        ga.across(2)
-        ga.to_partner(0)
+    with scope("ga_af1"):
+        ga.across_forward(-1)
+        ga.across_forward(1)
+    grad_relay(0)
+    grad_relay(1)
     with scope("gb_far"):
         gb.far()
         gb.across(2)
         gb.to_partner(0)
-    with scope("ga_af1"):
-        ga.across_forward(-1)
-        ga.across_forward(1)
-    def weight_part(ci, x_first):
-        cs = slice(ci * cols, (ci + 1) * cols)
+
+    def weight_part(first, *orders):
+        cs = slice(first * cols, (first + len(orders)) * cols)
 
         def step(xx, _):
             a = nt[xx, :, :, c].reshape(4 * rows, length)
             b = ntp[xx].reshape(4 * rows, length)
             acc = dot(a, hown[:, cs], NN) + dot(b, hpar[:, cs], NN)
             acc = acc.astype(BF16)
-            for ll in range(2):
-                for hh in range(2):
-                    yy, start = hh * 2 + ll, (ll * 2 + hh) * rows
-                    block = acc[start : start + rows]
-                    if x_first:
-                        part[ci, xx, yy] = block
-                    else:
-                        part[ci, yy, xx] = block
+            for i, x_first in enumerate(orders):
+                for ll in range(2):
+                    for hh in range(2):
+                        yy, start = hh * 2 + ll, (ll * 2 + hh) * rows
+                        block = acc[start : start + rows, i * cols : (i + 1) * cols]
+                        if x_first:
+                            part[first + i, xx, yy] = block
+                        else:
+                            part[first + i, yy, xx] = block
             return 0
 
         lax.fori_loop(0, 4, step, 0)
 
     class Scatter:
-        def __init__(self, ci, pa, to_a, pb, to_b):
+        def __init__(self, ci, pa, to_a, pb, to_b, to_far):
             self.ci, self.pa, self.to_a, self.pb, self.to_b = ci, pa, to_a, pb, to_b
+            self.to_far = to_far
             self.aup, self.adn, self.afar = m(pa + 1, 4), m(pa - 1, 4), m(pa + 2, 4)
             self.bup, self.bdn, self.bfar = m(pb + 1, 4), m(pb - 1, 4), m(pb + 2, 4)
 
@@ -308,40 +337,30 @@
             for j in range(4):
                 value = part[ci, self.pa, j].astype(F32) + rra[ci, 0, j].astype(F32)
                 rb[ci, j] = (value + rra[ci, 1, j].astype(F32)).astype(BF16)
-            self.g1 = [
-                send(rb.at[ci, self.bfar, lo], rb1.at[ci, 0], self.to_b[1]),
-                send(rb.at[ci, self.bfar, hi], rb1.at[ci, 1], self.to_b[-1]),
+            self.g2 = [
+                send(rb.at[ci, self.bfar], rrb.at[ci, 2], self.to_far),
+                send(rb.at[ci, self.bup], rrb.at[ci, 0], self.to_b[1]),
+                send(rb.at[ci, self.bdn], rrb.at[ci, 1], self.to_b[-1]),
             ]
-            self.g2 = [
-                send(rb.at[ci, self.bup, hi], rrb.at[ci, 0, hi], self.to_b[1]),
-                send(rb.at[ci, self.bdn, lo], rrb.at[ci, 1, lo], self.to_b[-1]),
-            ]
-
-        def fourth(self):
-            ci = self.ci
-            for i, (block, piece, device) in enumerate(
-                ((self.bup, lo, self.to_b[1]), (self.bdn, hi, self.to_b[-1]))
-            ):
-                self.g1[i].wait_recv()
-                old = rb[ci, block, piece].astype(F32)
-                rb[ci, block, piece] = (old + rb1[ci, i].astype(F32)).astype(BF16)
-                self.g2.append(send(rb.at[ci, block, piece], rrb.at[ci, i, piece], device))
 
         def finish(self, out):
             ci = self.ci
             for copy in self.g2:
                 copy.wait_recv()
             value = rb[ci, self.pb].astype(F32) + rrb[ci, 0].astype(F32)
-            out[...] = (value + rrb[ci, 1].astype(F32)) * (1.0 / 32.0)
-
-    rs_q = Scatter(0, x, to_x, y, to_y)
-    rs_k = Scatter(1, x, to_x, y, to_y)
-    rs_v = Scatter(2, y, to_y, x, to_x)
+            value = value + rrb[ci, 1].astype(F32) + rrb[ci, 2].astype(F32)
+            out[...] = value * (1.0 / 32.0)
+
+    y_far = at(x, m(y + 2, 4), c, z)
+    rs_q = Scatter(0, x, to_x, y, to_y, y_far)
+    rs_k = Scatter(1, x, to_x, y, to_y, y_far)
+    rs_v = Scatter(2, y, to_y, x, to_x, at(x_far, y, c, z))
 
     with scope("wp_q"):
         turned_copy.wait_recv()
         q_copy.wait_recv()
         weight_part(0, True)
+    grad_relay(2)
     with scope("ga_af2"):
         ga.across_forward(2)
         ga.to_partner(-1)
@@ -372,13 +391,16 @@
         ga.across_far(1)
     with scope("wp_v"):
         kv_copy.wait_recv()
-        weight_part(2, False)
+        weight_part(1, True, False)
     rs_v.first()
     with scope("ga_bf"):
         ga.across_far(2)
     with scope("gb_bf"):
         for ao in (0, -1, 1, 2):
             gb.across_far(ao)
+    with scope("q2"):
+        rs_q.second()
+    rs_k.first()
     with scope("wpar"):
         for group in (ga, gb):
             for copy in list(group.par.values()) + group.tail:
@@ -418,11 +440,6 @@
                 new.append(send(zb.at[j, whole], zr.at[i, 4 - step, whole], to_z[sign]))
             zs[p] = new
 
-    with scope("wp_k"):
-        weight_part(1, True)
-    with scope("q2"):
-        rs_q.second()
-    rs_k.first()
     z_block(3)
     z_step(3, 0)
     z_step(3, 1)
@@ -431,42 +448,50 @@
     z_block(2)
     with scope("q3"):
         rs_q.third()
+    with scope("k2"):
+        rs_k.second()
     z_step(2, 0)
     z_step(2, 1)
-    with scope("k2"):
-        rs_k.second()
     z_block(1)
     with scope("v3"):
         rs_v.third()
     z_step(1, 0)
-    with scope("q4"):
-        rs_q.fourth()
+    with scope("k3"):
+        rs_k.third()
     z_step(1, 1)
     last = input_block(z)
-    with scope("k3"):
-        rs_k.third()
-    with scope("v4"):
-        rs_v.fourth()
-    with scope("k4"):
-        rs_k.fourth()
     with scope("q5"):
         rs_q.finish(dq_out)
+        put(dq_out, dq_hbm, 0)
     with scope("v5"):
         rs_v.finish(dv_out)
+        put(dv_out, dv_hbm, 2)
     with scope("zlast"):
         for copies in zs:
             for copy in copies:
                 copy.wait_recv()
         dx_out[...] = (last + zr[0, 3].astype(F32) + zr[1, 3].astype(F32)).astype(BF16)
+        put(dx_out, dx_hbm, 3)
     with scope("k5"):
         rs_k.finish(dk_out)
+        put(dk_out, dk_hbm, 1)
+    for copy in stored:
+        copy.wait()
     for copy in started:
         copy.wait_send()
 
 
-def publish(a, b, c, d, oa, ob, oc, od):
-    for src, dst in ((a, oa), (b, ob), (c, oc), (d, od)):
-        dst[...] = src[...]
+def publish(*refs):
+    sources, targets, buffers, sem = refs[:4], refs[4:8], refs[8:12], refs[12]
+    reads = [pltpu.make_async_copy(sources[i], buffers[i], sem.at[i]) for i in range(4)]
+    writes = [pltpu.make_async_copy(buffers[i], targets[i], sem.at[4 + i]) for i in range(4)]
+    for copy in reads:
+        copy.start()
+    for read, write in zip(reads, writes):
+        read.wait()
+        write.start()
+    for copy in writes:
+        copy.wait()
 
 
 def body(normed, queries, keys, values, grads, links, wq, wk, wv):
@@ -486,10 +511,13 @@
             jax.ShapeDtypeStruct((rows, cols), F32),
         ),
         in_specs=[pl.BlockSpec(memory_space=pltpu.SMEM)] + [anywhere] * 8,
-        out_specs=(vmem,) * 4,
+        out_specs=(anywhere,) * 4,
         scratch_shapes=[
+            pltpu.VMEM((length, cols), BF16),
+            *[pltpu.VMEM((rows, cols), F32)] * 3,
             pltpu.VMEM((length, width), BF16),
             *[pltpu.VMEM((length, cols), BF16)] * 4,
+            pltpu.VMEM((2, 2, heads, length, HD), BF16),
             pltpu.VMEM((2, 2, heads, length, HD), BF16),
             pltpu.VMEM((4, 2, 2, 2, rows, 3 * cols), BF16),
             pltpu.VMEM((4, 2, 2, 2, rows, length), BF16),
@@ -503,8 +531,7 @@
             pltpu.VMEM((3, 2, 2, rows, cols), BF16),
             pltpu.VMEM((3, 2, 4, rows, cols), BF16),
             pltpu.VMEM((3, 4, rows, cols), BF16),
-            pltpu.VMEM((3, 2, rows // 2, cols), BF16),
-            pltpu.VMEM((3, 2, rows, cols), BF16),
+            pltpu.VMEM((3, 3, rows, cols), BF16),
             pltpu.VMEM((8, length, cols), BF16),
             pltpu.VMEM((2, 4, length, cols), BF16),
             pltpu.SemaphoreType.DMA((count,)),
@@ -524,8 +551,9 @@
     out = pl.pallas_call(
         publish,
         out_shape=[jax.ShapeDtypeStruct(o.shape, o.dtype) for o in out],
-        in_specs=[vmem] * 4,
-        out_specs=[vmem] * 4,
+        in_specs=[anywhere] * 4,
+        out_specs=[anywhere] * 4,
+        scratch_shapes=[pltpu.VMEM(o.shape, o.dtype) for o in out] + [pltpu.SemaphoreType.DMA((8,))],
         name="publish",
     )(*out)
     return (out[0].reshape(1, 1, length, cols), out[1], out[2], out[3])

time: 75.2 us -> 73.5 us (0.977)
  Pallas kernels: 74.3 us -> 72.2 us
    pallas_call x1, Pallas kernels: 72.4 us -> 70.3 us  [body(): pl.pallas_call(kernel, out_shape=(jax.ShapeDtypeStruct((length, cols), BF...]
where the time goes in v5:
time: 73.5 us; the launch traced here: 72.8 us
  Pallas kernels  72.2 us (98%)
    pallas_call x1, Pallas kernels, body(): pl.pallas_call(kernel, out_shape=(jax.ShapeDtypeStruct((length, cols), BF...  70.3 us
    pallas_call x1, Pallas kernels, body(): pl.pallas_call(publish, out_shape=[jax.ShapeDtypeStruct(o.shape, o.dtype)...  1.88 us

profile of v5, /device:TPU:1, one launch (start us, length us, event | category | flops | bytes accessed | tf_op | source)
XLA Modules:
  0.0 72.8 jit_solution(336898278433399866)
XLA Ops:
  0.6 70.3 %attention_backward.1 = (bf16[256,384]{1,0:T(8,128)(2,1)}, f32[96,384]{1,0:T(8,128)}, f32[96,384]{1,0:T(8,128)}, f32[96,384]{1,0:T(8,128)}) custom-call(s32[1,2]{1,0:T(1,128)} %links.1, bf16[256,3072]{1,0:T(8,128)(2,1)} %bitcast.6, bf16[256,384]{1,0:T(8,128)(2,1)} %bitcast.7, bf16[256,384]{1,0:T(8,128)(2,1)} %bitcast.8, bf16[256,384]{1,0:T(8,128)(2,1)} %bitcast.9, ...), custom_call_target="tpu_custom_call" | custom-call | tf_op jit(solution)/shard_map/attention_backward/pallas_call | solution.py:505
  70.9 1.9 %publish.1 = (bf16[256,384]{1,0:T(8,128)(2,1)}, f32[96,384]{1,0:T(8,128)}, f32[96,384]{1,0:T(8,128)}, f32[96,384]{1,0:T(8,128)}) custom-call(bf16[256,384]{1,0:T(8,128)(2,1)} %get-tuple-element.12.refs_0_, f32[96,384]{1,0:T(8,128)} %get-tuple-element.13.refs_1_, f32[96,384]{1,0:T(8,128)} %get-tuple-element.14.refs_2_, f32[96,384]{1,0:T(8,128)} %get-tuple-element.15.refs_3_), custom_call_target="tpu_custom_call" | custom-call | tf_op jit(solution)/shard_map/publish/pallas_call | solution.py:551

commit v6 on v5

--- a/solution.py
+++ b/solution.py
@@ -109,18 +109,12 @@
     with scope("barrier"):
         pl.semaphore_wait(barrier, len(peers))
 
-    turn = 1 - 2 * yh
-    to_turn = at(m(x + turn, 4), y, c, z)
-
     class Gather:
         def __init__(self, start, size, x_first):
             self.x_first = x_first
             self.all = pl.ds(start, size)
             self.to_a, self.to_b = (to_x, to_y) if x_first else (to_y, to_x)
             self.half = (pl.ds(start, size // 2), pl.ds(start + size // 2, size // 2))
-            side = size // 4
-            self.outer = (pl.ds(start, side), pl.ds(start + size - side, side))
-            self.inner = pl.ds(start + side, size - 2 * side)
             self.b1, self.b2, self.par, self.tail = {}, {}, {}, []
 
         def ref(self, ao, bo, piece):
@@ -141,10 +135,7 @@
         def forward(self):
             for copy in self.a1:
                 copy.wait_recv()
-            if self.x_first:
-                self.a2 = [self.pass_on(-turn, 0, self.all, to_turn)]
-            else:
-                self.a2 = [self.pass_on(-s, 0, self.half[i], self.to_a[s]) for i, s in enumerate((1, -1))]
+            self.a2 = [self.pass_on(-s, 0, self.half[i], self.to_a[s]) for i, s in enumerate((1, -1))]
 
         def far(self):
             for copy in self.a2:
@@ -153,11 +144,7 @@
         def across_forward(self, ao):
             for copy in self.b1[ao]:
                 copy.wait_recv()
-            if self.x_first:
-                self.b2[ao] = [self.pass_on(ao, -s, self.half[i], self.to_b[s]) for i, s in enumerate((1, -1))]
-            else:
-                self.b2[ao] = [self.pass_on(ao, -s, self.outer[i], self.to_b[s]) for i, s in enumerate((1, -1))]
-                self.b2[ao].append(self.pass_on(ao, -turn, self.inner, to_turn))
+            self.b2[ao] = [self.pass_on(ao, -s, self.half[i], self.to_b[s]) for i, s in enumerate((1, -1))]
 
         def across_far(self, ao):
             for copy in self.b2[ao]:
@@ -441,11 +428,11 @@
             zs[p] = new
 
     z_block(3)
+    z_block(2)
     z_step(3, 0)
     z_step(3, 1)
     with scope("v2"):
         rs_v.second()
-    z_block(2)
     with scope("q3"):
         rs_q.third()
     with scope("k2"):

time: 73.5 us -> 72.4 us (0.985)
  no operation moved by 1% of the time
where the time goes in v6:
time: 72.4 us; the launch traced here: 72.2 us
  Pallas kernels  71.6 us (99%)
    pallas_call x1, Pallas kernels, body(): pl.pallas_call(kernel, out_shape=(jax.ShapeDtypeStruct((length, cols), BF...  69.7 us
    pallas_call x1, Pallas kernels, body(): pl.pallas_call(publish, out_shape=[jax.ShapeDtypeStruct(o.shape, o.dtype)...  1.88 us

profile of v6, /device:TPU:1, one launch (start us, length us, event | category | flops | bytes accessed | tf_op | source)
XLA Modules:
  0.0 72.2 jit_solution(18234118115631926398)
XLA Ops:
  0.6 69.7 %attention_backward.1 = (bf16[256,384]{1,0:T(8,128)(2,1)}, f32[96,384]{1,0:T(8,128)}, f32[96,384]{1,0:T(8,128)}, f32[96,384]{1,0:T(8,128)}) custom-call(s32[1,2]{1,0:T(1,128)} %links.1, bf16[256,3072]{1,0:T(8,128)(2,1)} %bitcast.6, bf16[256,384]{1,0:T(8,128)(2,1)} %bitcast.7, bf16[256,384]{1,0:T(8,128)(2,1)} %bitcast.8, bf16[256,384]{1,0:T(8,128)(2,1)} %bitcast.9, ...), custom_call_target="tpu_custom_call" | custom-call | tf_op jit(solution)/shard_map/attention_backward/pallas_call | solution.py:492
  70.4 1.9 %publish.1 = (bf16[256,384]{1,0:T(8,128)(2,1)}, f32[96,384]{1,0:T(8,128)}, f32[96,384]{1,0:T(8,128)}, f32[96,384]{1,0:T(8,128)}) custom-call(bf16[256,384]{1,0:T(8,128)(2,1)} %get-tuple-element.12.refs_0_, f32[96,384]{1,0:T(8,128)} %get-tuple-element.13.refs_1_, f32[96,384]{1,0:T(8,128)} %get-tuple-element.14.refs_2_, f32[96,384]{1,0:T(8,128)} %get-tuple-element.15.refs_3_), custom_call_target="tpu_custom_call" | custom-call | tf_op jit(solution)/shard_map/publish/pallas_call | solution.py:538

commit v7 on v6

--- a/solution.py
+++ b/solution.py
@@ -437,9 +437,9 @@
         rs_q.third()
     with scope("k2"):
         rs_k.second()
+    z_block(1)
     z_step(2, 0)
     z_step(2, 1)
-    z_block(1)
     with scope("v3"):
         rs_v.third()
     z_step(1, 0)

time: 72.4 us -> 72.3 us (level)
  no operation moved by 1% of the time
where the time goes in v7:
time: 72.3 us; the launch traced here: 71.9 us
  Pallas kernels  71.2 us (98%)
    pallas_call x1, Pallas kernels, body(): pl.pallas_call(kernel, out_shape=(jax.ShapeDtypeStruct((length, cols), BF...  69.4 us
    pallas_call x1, Pallas kernels, body(): pl.pallas_call(publish, out_shape=[jax.ShapeDtypeStruct(o.shape, o.dtype)...  1.88 us

profile of v7, /device:TPU:1, one launch (start us, length us, event | category | flops | bytes accessed | tf_op | source)
XLA Modules:
  0.0 71.9 jit_solution(11876183545779111345)
XLA Ops:
  0.6 69.4 %attention_backward.1 = (bf16[256,384]{1,0:T(8,128)(2,1)}, f32[96,384]{1,0:T(8,128)}, f32[96,384]{1,0:T(8,128)}, f32[96,384]{1,0:T(8,128)}) custom-call(s32[1,2]{1,0:T(1,128)} %links.1, bf16[256,3072]{1,0:T(8,128)(2,1)} %bitcast.6, bf16[256,384]{1,0:T(8,128)(2,1)} %bitcast.7, bf16[256,384]{1,0:T(8,128)(2,1)} %bitcast.8, bf16[256,384]{1,0:T(8,128)(2,1)} %bitcast.9, ...), custom_call_target="tpu_custom_call" | custom-call | tf_op jit(solution)/shard_map/attention_backward/pallas_call | solution.py:492
  70.0 1.9 %publish.1 = (bf16[256,384]{1,0:T(8,128)(2,1)}, f32[96,384]{1,0:T(8,128)}, f32[96,384]{1,0:T(8,128)}, f32[96,384]{1,0:T(8,128)}) custom-call(bf16[256,384]{1,0:T(8,128)(2,1)} %get-tuple-element.12.refs_0_, f32[96,384]{1,0:T(8,128)} %get-tuple-element.13.refs_1_, f32[96,384]{1,0:T(8,128)} %get-tuple-element.14.refs_2_, f32[96,384]{1,0:T(8,128)} %get-tuple-element.15.refs_3_), custom_call_target="tpu_custom_call" | custom-call | tf_op jit(solution)/shard_map/publish/pallas_call | solution.py:538
